TPU v7x, 32 devices: a whole 2x2x4 slice. The times are simulated.
32 devices in a mesh: net: 8 (over z, x), tm: 4 (over y, core).
Axes of the slice: x: 2, y: 2, z: 4, core: 2. Of those that a mesh axis runs over, the one named last changes fastest.
Arguments:
- initial: float32 [3, 128, 1024], P(None, 'net'), may hold values from -6 to 6
- wall_drag_factor: float32 [128], P('net'), may hold values from 0.05 to 0.5
- ground_exchange_rate: float32 [128], P('net'), may hold values from 0.02 to 0.3
- send_ends: int32 [8, 8, 8], P('net'), may hold values from -1 to 31, as said below
- recv_junction: int32 [8, 8, 8], P('net'), may hold values from -1 to 7, as said below
- slab_steps: int32 [4], P('tm'), may hold values from 4 to 8, as said below
Outputs:
- slab_ends: float32 [4, 3, 128, 1024], P('tm', None, 'net')
Inputs may be any that keep to these rules, and one draw needn't show every extreme that they name: `send_ends`: entry [k, d, s] is an end of partition k whose junction partition d owns, or -1; the live entries of each list come first, every end of a partition appears exactly once in its lists, and in every draw each partition has one list to some owner that fills all 8 slots; each owner receives exactly 32 ends in all. `recv_junction`: entry [d, k, s] is live exactly where send_ends[k, d, s] is, and then names the owner-local junction of that end; every junction of every owner has at least one end. `slab_steps`: some slab takes 4 fine steps and some 2 * 4.
All inputs are finite; a program needn't handle non-finite values.
Results may differ from a plain program's by a relative error of at most 0.0001.
Values sent between devices are 32-bit elements; how exact they have to be, the bound alone decides.
A program may use at most 64 MiB of HBM per device.

v0:
```python
import jax
import jax.numpy as jnp
from jax import lax
from jax.sharding import PartitionSpec as P

STEPS_MAX = 8


def passed_along(value, axis, steps):
    count = lax.axis_size(axis)
    leading, last = (max(0, -steps), min(count, count - steps))
    return lax.ppermute(value, axis, [(source, source + steps) for source in range(leading, last)])


def advect_quantity(
    state_buffers,
    entering_upstream,
    entering_downstream,
    upstream_warmth,
    downstream_warmth,
    clock_delta,
    wall_drag_factor,
    ground_exchange_rate,
):
    pressure = state_buffers[0]
    mass_flux = state_buffers[1]
    volume_heat_level = state_buffers[2]
    right_wave = pressure + mass_flux
    left_wave = pressure - mass_flux
    right_prev = jnp.concatenate([entering_upstream[:, None], right_wave[:, :-1]], 1)
    left_next = jnp.concatenate([left_wave[:, 1:], entering_downstream[:, None]], 1)
    right_new = right_wave - clock_delta * (right_wave - right_prev)
    left_new = left_wave - clock_delta * (left_wave - left_next)
    flux_star = 0.5 * (right_new - left_new)
    press_new = 0.5 * (right_new + left_new)
    flux_new = flux_star / (1.0 + clock_delta * wall_drag_factor[:, None] * jnp.abs(flux_star))
    stream_velocity = mass_flux / (1.0 + jnp.abs(mass_flux))
    prior_warmth = jnp.concatenate([upstream_warmth[:, None], volume_heat_level[:, :-1]], 1)
    coming_warmth = jnp.concatenate([volume_heat_level[:, 1:], downstream_warmth[:, None]], 1)
    carried_entries = volume_heat_level - clock_delta * (
        jnp.maximum(stream_velocity, 0.0) * (volume_heat_level - prior_warmth)
        + jnp.minimum(stream_velocity, 0.0) * (coming_warmth - volume_heat_level)
    )
    temp_new = carried_entries / (1.0 + clock_delta * ground_exchange_rate[:, None])
    return jnp.stack([press_new, flux_new, temp_new], 0)


def body(initial, wall_drag_factor, ground_exchange_rate, send_ends, recv_junction, slab_steps):
    parts = lax.axis_size("net")
    slabs = lax.axis_size("tm")
    slab_index = lax.axis_index("tm")
    pipes = initial.shape[1]
    ends_dev = 2 * pipes
    junctions = pipes // 2
    slot_count = send_ends.shape[2]
    highest = lax.Precision.HIGHEST
    send_table = send_ends[0].reshape(-1)
    send_onehot = (send_table[:, None] == jnp.arange(ends_dev, dtype=jnp.int32)[None, :]).astype(
        jnp.float32
    )
    recv_table = recv_junction[0].reshape(-1)
    recv_onehot = (jnp.arange(junctions, dtype=jnp.int32)[:, None] == recv_table[None, :]).astype(
        jnp.float32
    )
    degree = jnp.sum(recv_onehot, axis=1)

    def attach_nodes(state_buffers):
        pressure = state_buffers[0]
        mass_flux = state_buffers[1]
        volume_heat_level = state_buffers[2]
        departing_signal = jnp.concatenate(
            [pressure[:, 0] - mass_flux[:, 0], pressure[:, -1] + mass_flux[:, -1]]
        )
        exit_warmth = jnp.concatenate([volume_heat_level[:, 0], volume_heat_level[:, -1]])
        local_entries = jnp.stack([departing_signal, exit_warmth], 1)
        outbound = jnp.dot(send_onehot, local_entries, precision=highest)
        inbound = lax.all_to_all(
            outbound.reshape(parts, slot_count, 2), "net", split_axis=0, concat_axis=0, tiled=True
        ).reshape(-1, 2)
        means = jnp.dot(recv_onehot, inbound, precision=highest) / degree[:, None]
        slot_means = jnp.dot(recv_onehot.T, means, precision=highest)
        reply = jnp.stack([2.0 * slot_means[:, 0] - inbound[:, 0], slot_means[:, 1]], 1).reshape(
            parts, slot_count, 2
        )
        returned = lax.all_to_all(reply, "net", split_axis=0, concat_axis=0, tiled=True).reshape(
            -1, 2
        )
        ghosts = jnp.dot(send_onehot.T, returned, precision=highest)
        return (ghosts[:pipes, 0], ghosts[pipes:, 0], ghosts[:pipes, 1], ghosts[pipes:, 1])

    def advance(state_buffers, clock_delta):
        entering_upstream, entering_downstream, upstream_warmth, downstream_warmth = attach_nodes(
            state_buffers
        )
        return advect_quantity(
            state_buffers,
            entering_upstream,
            entering_downstream,
            upstream_warmth,
            downstream_warmth,
            clock_delta,
            wall_drag_factor,
            ground_exchange_rate,
        )

    def coarse(state_buffers):
        return advance(state_buffers, jnp.float32(1.0))

    def sweep(correction):

        def relay_section(section_no, loop_carry):
            current, own_coarse = loop_carry
            coarse_end = coarse(current)
            candidate = coarse_end if correction is None else coarse_end + correction
            passed = passed_along(candidate, "tm", 1)
            own_coarse = jnp.where(slab_index == section_no, coarse_end, own_coarse)
            current = jnp.where(slab_index == section_no + 1, passed, current)
            return (current, own_coarse)

        own_start, own_coarse = lax.fori_loop(
            0, slabs, relay_section, (initial, jnp.zeros_like(initial))
        )
        return (own_start, own_coarse)

    start_now, coarse_now = sweep(None)
    correction = jnp.zeros_like(initial)
    step_count = slab_steps[0]
    clock_delta = jnp.float32(1.0) / step_count.astype(jnp.float32)

    def masked_step(step_no, current):
        return jnp.where(step_no < step_count, advance(current, clock_delta), current)

    fine_end = lax.fori_loop(0, STEPS_MAX, masked_step, start_now)
    correction = fine_end - coarse_now
    start_now, coarse_now = sweep(correction)
    return (coarse_now + correction)[None]


def solution(mesh):
    return jax.shard_map(
        body,
        mesh=mesh,
        in_specs=(
            P(None, "net", None),
            P("net"),
            P("net"),
            P("net", None, None),
            P("net", None, None),
            P("tm"),
        ),
        out_specs=P("tm", None, "net", None),
        check_vma=False,
    )
```

profile of v0, /device:TPU:5, one launch (start us, length us, event | category | flops | bytes accessed | tf_op | source)
XLA Modules:
  0.0 429.0 jit_solution(2733909461873683528)
XLA Ops:
  2.4 119.6 %while.47 = (s32[]{:T(128)}, f32[3,16,1024]{2,1,0:T(8,128)S(1)}, f32[3,16,1024]{2,1,0:T(8,128)S(1)}, s32[]{:T(128)}, f32[8]{0:T(128)S(1)}, /*index=5*/f32[16]{0:...) while((s32[]{:T(128)}, f32[3,16,1024]{2,1,0:T(8,128)S(1)}, ...), condition=%wide.region_2.3_spmd.clone, body=%wide.region_1.2_spmd.clone.sunk | while | flops 903589 | bytes 4178835 | solution.py:120
  3.7 5.5 %all-to-all-start.2 = ((f32[8,8,2]{1,2,0:T(2,128)}), f32[8,8,2]{1,2,0:T(2,128)S(1)}, u32[]{:S(2)}, u32[]{:S(2)}) async-start(f32[8,8,2]{1,2,0:T(2,128)} %copy.117), calls=%async_computation.2 | async-start | bytes 16384 | tf_op jit(solution)/shard_map/while/body/eval_jaxpr/all_to_all | solution.py:77
  9.4 5.2 %all-to-all-done.2 = f32[8,8,2]{1,2,0:T(2,128)S(1)} async-done(((f32[8,8,2]{1,2,0:T(2,128)}), f32[8,8,2]{1,2,0:T(2,128)S(1)}, u32[]{:S(2)}, u32[]{:S(2)}) %all-to-all-start.2) | async-done | bytes 544 | tf_op jit(solution)/shard_map/while/body/eval_jaxpr/all_to_all | solution.py:77
  15.8 3.3 all-to-all-start.3
  19.2 5.3 %all-to-all-done.3 = f32[8,8,2]{1,2,0:T(2,128)S(1)} async-done(((f32[8,8,2]{1,2,0:T(2,128)}), f32[8,8,2]{1,2,0:T(2,128)S(1)}, u32[]{:S(2)}, u32[]{:S(2)}) %all-to-all-start.3) | async-done | bytes 544 | tf_op jit(solution)/shard_map/while/body/eval_jaxpr/all_to_all | solution.py:85
  26.8 4.8 %collective-permute-done = f32[3,16,1024]{2,1,0:T(8,128)S(1)} collective-permute-done((f32[3,16,1024]{2,1,0:T(8,128)S(1)}, f32[3,16,1024]{2,1,0:T(8,128)S(1)}, u32[]{:S(2)}, u32[]{:S(2)}) %collective-permute-start) | collective-permute-done | bytes 196640 | tf_op jit(solution)/shard_map/while/body/eval_jaxpr/ppermute | solution.py:12
  32.9 3.3 all-to-all-start.2
  36.4 5.2 %all-to-all-done.2 = f32[8,8,2]{1,2,0:T(2,128)S(1)} async-done(((f32[8,8,2]{1,2,0:T(2,128)}), f32[8,8,2]{1,2,0:T(2,128)S(1)}, u32[]{:S(2)}, u32[]{:S(2)}) %all-to-all-start.2) | async-done | bytes 544 | tf_op jit(solution)/shard_map/while/body/eval_jaxpr/all_to_all | solution.py:77
  46.1 5.3 %all-to-all-done.3 = f32[8,8,2]{1,2,0:T(2,128)S(1)} async-done(((f32[8,8,2]{1,2,0:T(2,128)}), f32[8,8,2]{1,2,0:T(2,128)S(1)}, u32[]{:S(2)}, u32[]{:S(2)}) %all-to-all-start.3) | async-done | bytes 544 | tf_op jit(solution)/shard_map/while/body/eval_jaxpr/all_to_all | solution.py:85
  53.7 8.0 %collective-permute-done = f32[3,16,1024]{2,1,0:T(8,128)S(1)} collective-permute-done((f32[3,16,1024]{2,1,0:T(8,128)S(1)}, f32[3,16,1024]{2,1,0:T(8,128)S(1)}, u32[]{:S(2)}, u32[]{:S(2)}) %collective-permute-start) | collective-permute-done | bytes 196640 | tf_op jit(solution)/shard_map/while/body/eval_jaxpr/ppermute | solution.py:12
  66.6 5.2 %all-to-all-done.2 = f32[8,8,2]{1,2,0:T(2,128)S(1)} async-done(((f32[8,8,2]{1,2,0:T(2,128)}), f32[8,8,2]{1,2,0:T(2,128)S(1)}, u32[]{:S(2)}, u32[]{:S(2)}) %all-to-all-start.2) | async-done | bytes 544 | tf_op jit(solution)/shard_map/while/body/eval_jaxpr/all_to_all | solution.py:77
  72.9 3.3 all-to-all-start.3
  76.3 5.3 %all-to-all-done.3 = f32[8,8,2]{1,2,0:T(2,128)S(1)} async-done(((f32[8,8,2]{1,2,0:T(2,128)}), f32[8,8,2]{1,2,0:T(2,128)S(1)}, u32[]{:S(2)}, u32[]{:S(2)}) %all-to-all-start.3) | async-done | bytes 544 | tf_op jit(solution)/shard_map/while/body/eval_jaxpr/all_to_all | solution.py:85
  83.9 8.0 %collective-permute-done = f32[3,16,1024]{2,1,0:T(8,128)S(1)} collective-permute-done((f32[3,16,1024]{2,1,0:T(8,128)S(1)}, f32[3,16,1024]{2,1,0:T(8,128)S(1)}, u32[]{:S(2)}, u32[]{:S(2)}) %collective-permute-start) | collective-permute-done | bytes 196640 | tf_op jit(solution)/shard_map/while/body/eval_jaxpr/ppermute | solution.py:12
  96.7 5.2 %all-to-all-done.2 = f32[8,8,2]{1,2,0:T(2,128)S(1)} async-done(((f32[8,8,2]{1,2,0:T(2,128)}), f32[8,8,2]{1,2,0:T(2,128)S(1)}, u32[]{:S(2)}, u32[]{:S(2)}) %all-to-all-start.2) | async-done | bytes 544 | tf_op jit(solution)/shard_map/while/body/eval_jaxpr/all_to_all | solution.py:77
  106.4 5.3 %all-to-all-done.3 = f32[8,8,2]{1,2,0:T(2,128)S(1)} async-done(((f32[8,8,2]{1,2,0:T(2,128)}), f32[8,8,2]{1,2,0:T(2,128)S(1)}, u32[]{:S(2)}, u32[]{:S(2)}) %all-to-all-start.3) | async-done | bytes 544 | tf_op jit(solution)/shard_map/while/body/eval_jaxpr/all_to_all | solution.py:85
  114.0 8.0 %collective-permute-done = f32[3,16,1024]{2,1,0:T(8,128)S(1)} collective-permute-done((f32[3,16,1024]{2,1,0:T(8,128)S(1)}, f32[3,16,1024]{2,1,0:T(8,128)S(1)}, u32[]{:S(2)}, u32[]{:S(2)}) %collective-permute-start) | collective-permute-done | bytes 196640 | tf_op jit(solution)/shard_map/while/body/eval_jaxpr/ppermute | solution.py:12
  122.7 166.4 %while.46 = (s32[]{:T(128)}, f32[3,16,1024]{2,1,0:T(8,128)S(1)}, s32[]{:T(128)}, f32[]{:T(128)}, f32[8]{0:T(128)S(1)}, /*index=5*/f32[16]{0:T(128)S(1)}, f32[16]...) while((s32[]{:T(128)}, f32[3,16,1024]{2,1,0:T(8,128)S(1)}, s32[]{:T(128)}, f32[]{:T(128)}, ...), condition=%wide.region_4.5_spmd.clone, body=%wide.region_3.4_spmd.clone.sunk | while | flops 854467 | bytes 2606039 | solution.py:133
  127.5 5.2 %all-to-all-done = f32[8,8,2]{1,2,0:T(2,128)S(1)} async-done(((f32[8,8,2]{1,2,0:T(2,128)}), f32[8,8,2]{1,2,0:T(2,128)S(1)}, u32[]{:S(2)}, u32[]{:S(2)}) %all-to-all-start) | async-done | bytes 544 | tf_op jit(solution)/shard_map/while/body/eval_jaxpr/all_to_all | solution.py:77
  137.9 4.6 %all-to-all-done.1 = f32[8,8,2]{1,2,0:T(2,128)S(1)} async-done(((f32[8,8,2]{1,2,0:T(2,128)}), f32[8,8,2]{1,2,0:T(2,128)S(1)}, u32[]{:S(2)}, u32[]{:S(2)}) %all-to-all-start.1) | async-done | bytes 544 | tf_op jit(solution)/shard_map/while/body/eval_jaxpr/all_to_all | solution.py:85
  148.3 5.2 %all-to-all-done = f32[8,8,2]{1,2,0:T(2,128)S(1)} async-done(((f32[8,8,2]{1,2,0:T(2,128)}), f32[8,8,2]{1,2,0:T(2,128)S(1)}, u32[]{:S(2)}, u32[]{:S(2)}) %all-to-all-start) | async-done | bytes 544 | tf_op jit(solution)/shard_map/while/body/eval_jaxpr/all_to_all | solution.py:77
  158.7 4.6 %all-to-all-done.1 = f32[8,8,2]{1,2,0:T(2,128)S(1)} async-done(((f32[8,8,2]{1,2,0:T(2,128)}), f32[8,8,2]{1,2,0:T(2,128)S(1)}, u32[]{:S(2)}, u32[]{:S(2)}) %all-to-all-start.1) | async-done | bytes 544 | tf_op jit(solution)/shard_map/while/body/eval_jaxpr/all_to_all | solution.py:85
  169.1 5.2 %all-to-all-done = f32[8,8,2]{1,2,0:T(2,128)S(1)} async-done(((f32[8,8,2]{1,2,0:T(2,128)}), f32[8,8,2]{1,2,0:T(2,128)S(1)}, u32[]{:S(2)}, u32[]{:S(2)}) %all-to-all-start) | async-done | bytes 544 | tf_op jit(solution)/shard_map/while/body/eval_jaxpr/all_to_all | solution.py:77
  179.5 4.6 %all-to-all-done.1 = f32[8,8,2]{1,2,0:T(2,128)S(1)} async-done(((f32[8,8,2]{1,2,0:T(2,128)}), f32[8,8,2]{1,2,0:T(2,128)S(1)}, u32[]{:S(2)}, u32[]{:S(2)}) %all-to-all-start.1) | async-done | bytes 544 | tf_op jit(solution)/shard_map/while/body/eval_jaxpr/all_to_all | solution.py:85
  189.9 5.2 %all-to-all-done = f32[8,8,2]{1,2,0:T(2,128)S(1)} async-done(((f32[8,8,2]{1,2,0:T(2,128)}), f32[8,8,2]{1,2,0:T(2,128)S(1)}, u32[]{:S(2)}, u32[]{:S(2)}) %all-to-all-start) | async-done | bytes 544 | tf_op jit(solution)/shard_map/while/body/eval_jaxpr/all_to_all | solution.py:77
  200.3 4.6 %all-to-all-done.1 = f32[8,8,2]{1,2,0:T(2,128)S(1)} async-done(((f32[8,8,2]{1,2,0:T(2,128)}), f32[8,8,2]{1,2,0:T(2,128)S(1)}, u32[]{:S(2)}, u32[]{:S(2)}) %all-to-all-start.1) | async-done | bytes 544 | tf_op jit(solution)/shard_map/while/body/eval_jaxpr/all_to_all | solution.py:85
  210.7 5.2 %all-to-all-done = f32[8,8,2]{1,2,0:T(2,128)S(1)} async-done(((f32[8,8,2]{1,2,0:T(2,128)}), f32[8,8,2]{1,2,0:T(2,128)S(1)}, u32[]{:S(2)}, u32[]{:S(2)}) %all-to-all-start) | async-done | bytes 544 | tf_op jit(solution)/shard_map/while/body/eval_jaxpr/all_to_all | solution.py:77
  221.1 4.6 %all-to-all-done.1 = f32[8,8,2]{1,2,0:T(2,128)S(1)} async-done(((f32[8,8,2]{1,2,0:T(2,128)}), f32[8,8,2]{1,2,0:T(2,128)S(1)}, u32[]{:S(2)}, u32[]{:S(2)}) %all-to-all-start.1) | async-done | bytes 544 | tf_op jit(solution)/shard_map/while/body/eval_jaxpr/all_to_all | solution.py:85
  231.5 5.2 %all-to-all-done = f32[8,8,2]{1,2,0:T(2,128)S(1)} async-done(((f32[8,8,2]{1,2,0:T(2,128)}), f32[8,8,2]{1,2,0:T(2,128)S(1)}, u32[]{:S(2)}, u32[]{:S(2)}) %all-to-all-start) | async-done | bytes 544 | tf_op jit(solution)/shard_map/while/body/eval_jaxpr/all_to_all | solution.py:77
  241.9 4.6 %all-to-all-done.1 = f32[8,8,2]{1,2,0:T(2,128)S(1)} async-done(((f32[8,8,2]{1,2,0:T(2,128)}), f32[8,8,2]{1,2,0:T(2,128)S(1)}, u32[]{:S(2)}, u32[]{:S(2)}) %all-to-all-start.1) | async-done | bytes 544 | tf_op jit(solution)/shard_map/while/body/eval_jaxpr/all_to_all | solution.py:85
  252.3 5.2 %all-to-all-done = f32[8,8,2]{1,2,0:T(2,128)S(1)} async-done(((f32[8,8,2]{1,2,0:T(2,128)}), f32[8,8,2]{1,2,0:T(2,128)S(1)}, u32[]{:S(2)}, u32[]{:S(2)}) %all-to-all-start) | async-done | bytes 544 | tf_op jit(solution)/shard_map/while/body/eval_jaxpr/all_to_all | solution.py:77
  262.7 4.6 %all-to-all-done.1 = f32[8,8,2]{1,2,0:T(2,128)S(1)} async-done(((f32[8,8,2]{1,2,0:T(2,128)}), f32[8,8,2]{1,2,0:T(2,128)S(1)}, u32[]{:S(2)}, u32[]{:S(2)}) %all-to-all-start.1) | async-done | bytes 544 | tf_op jit(solution)/shard_map/while/body/eval_jaxpr/all_to_all | solution.py:85
  273.1 5.2 %all-to-all-done = f32[8,8,2]{1,2,0:T(2,128)S(1)} async-done(((f32[8,8,2]{1,2,0:T(2,128)}), f32[8,8,2]{1,2,0:T(2,128)S(1)}, u32[]{:S(2)}, u32[]{:S(2)}) %all-to-all-start) | async-done | bytes 544 | tf_op jit(solution)/shard_map/while/body/eval_jaxpr/all_to_all | solution.py:77
  283.5 4.6 %all-to-all-done.1 = f32[8,8,2]{1,2,0:T(2,128)S(1)} async-done(((f32[8,8,2]{1,2,0:T(2,128)}), f32[8,8,2]{1,2,0:T(2,128)S(1)}, u32[]{:S(2)}, u32[]{:S(2)}) %all-to-all-start.1) | async-done | bytes 544 | tf_op jit(solution)/shard_map/while/body/eval_jaxpr/all_to_all | solution.py:85
  289.2 139.1 %while.48 = (s32[]{:T(128)}, f32[3,16,1024]{2,1,0:T(8,128)S(1)}, f32[3,16,1024]{2,1,0:T(8,128)S(1)}, s32[]{:T(128)}, f32[8]{0:T(128)S(1)}, /*index=5*/f32[16]{0:...) while((s32[]{:T(128)}, f32[3,16,1024]{2,1,0:T(8,128)S(1)}, ...), condition=%wide.region_6.7_spmd.clone, body=%wide.region_5.6_spmd.clone.sunk | while | flops 952741 | bytes 4375451 | solution.py:120
  294.0 5.3 %all-to-all-done.4 = f32[8,8,2]{1,2,0:T(2,128)S(1)} async-done(((f32[8,8,2]{1,2,0:T(2,128)}), f32[8,8,2]{1,2,0:T(2,128)S(1)}, u32[]{:S(2)}, u32[]{:S(2)}) %all-to-all-start.4) | async-done | bytes 544 | tf_op jit(solution)/shard_map/while/body/eval_jaxpr/all_to_all | solution.py:77
  303.9 5.3 %all-to-all-done.5 = f32[8,8,2]{1,2,0:T(2,128)S(1)} async-done(((f32[8,8,2]{1,2,0:T(2,128)}), f32[8,8,2]{1,2,0:T(2,128)S(1)}, u32[]{:S(2)}, u32[]{:S(2)}) %all-to-all-start.5) | async-done | bytes 544 | tf_op jit(solution)/shard_map/while/body/eval_jaxpr/all_to_all | solution.py:85
  311.5 26.2 %collective-permute-done.1 = f32[3,16,1024]{2,1,0:T(8,128)S(1)} collective-permute-done((f32[3,16,1024]{2,1,0:T(8,128)S(1)}, f32[3,16,1024]{2,1,0:T(8,128)S(1)}, u32[]{:S(2)}, u32[]{:S(2)}) %collective-permute-start.1) | collective-permute-done | bytes 196640 | tf_op jit(solution)/shard_map/while/body/eval_jaxpr/ppermute | solution.py:12
  342.6 5.2 %all-to-all-done.4 = f32[8,8,2]{1,2,0:T(2,128)S(1)} async-done(((f32[8,8,2]{1,2,0:T(2,128)}), f32[8,8,2]{1,2,0:T(2,128)S(1)}, u32[]{:S(2)}, u32[]{:S(2)}) %all-to-all-start.4) | async-done | bytes 544 | tf_op jit(solution)/shard_map/while/body/eval_jaxpr/all_to_all | solution.py:77
  352.3 5.3 %all-to-all-done.5 = f32[8,8,2]{1,2,0:T(2,128)S(1)} async-done(((f32[8,8,2]{1,2,0:T(2,128)}), f32[8,8,2]{1,2,0:T(2,128)S(1)}, u32[]{:S(2)}, u32[]{:S(2)}) %all-to-all-start.5) | async-done | bytes 544 | tf_op jit(solution)/shard_map/while/body/eval_jaxpr/all_to_all | solution.py:85
  359.9 8.0 %collective-permute-done.1 = f32[3,16,1024]{2,1,0:T(8,128)S(1)} collective-permute-done((f32[3,16,1024]{2,1,0:T(8,128)S(1)}, f32[3,16,1024]{2,1,0:T(8,128)S(1)}, u32[]{:S(2)}, u32[]{:S(2)}) %collective-permute-start.1) | collective-permute-done | bytes 196640 | tf_op jit(solution)/shard_map/while/body/eval_jaxpr/ppermute | solution.py:12
  372.8 5.2 %all-to-all-done.4 = f32[8,8,2]{1,2,0:T(2,128)S(1)} async-done(((f32[8,8,2]{1,2,0:T(2,128)}), f32[8,8,2]{1,2,0:T(2,128)S(1)}, u32[]{:S(2)}, u32[]{:S(2)}) %all-to-all-start.4) | async-done | bytes 544 | tf_op jit(solution)/shard_map/while/body/eval_jaxpr/all_to_all | solution.py:77
  379.1 3.3 all-to-all-start.5
  382.5 5.3 %all-to-all-done.5 = f32[8,8,2]{1,2,0:T(2,128)S(1)} async-done(((f32[8,8,2]{1,2,0:T(2,128)}), f32[8,8,2]{1,2,0:T(2,128)S(1)}, u32[]{:S(2)}, u32[]{:S(2)}) %all-to-all-start.5) | async-done | bytes 544 | tf_op jit(solution)/shard_map/while/body/eval_jaxpr/all_to_all | solution.py:85
  390.1 8.0 %collective-permute-done.1 = f32[3,16,1024]{2,1,0:T(8,128)S(1)} collective-permute-done((f32[3,16,1024]{2,1,0:T(8,128)S(1)}, f32[3,16,1024]{2,1,0:T(8,128)S(1)}, u32[]{:S(2)}, u32[]{:S(2)}) %collective-permute-start.1) | collective-permute-done | bytes 196640 | tf_op jit(solution)/shard_map/while/body/eval_jaxpr/ppermute | solution.py:12
  402.9 5.2 %all-to-all-done.4 = f32[8,8,2]{1,2,0:T(2,128)S(1)} async-done(((f32[8,8,2]{1,2,0:T(2,128)}), f32[8,8,2]{1,2,0:T(2,128)S(1)}, u32[]{:S(2)}, u32[]{:S(2)}) %all-to-all-start.4) | async-done | bytes 544 | tf_op jit(solution)/shard_map/while/body/eval_jaxpr/all_to_all | solution.py:77
  412.7 5.3 %all-to-all-done.5 = f32[8,8,2]{1,2,0:T(2,128)S(1)} async-done(((f32[8,8,2]{1,2,0:T(2,128)}), f32[8,8,2]{1,2,0:T(2,128)S(1)}, u32[]{:S(2)}, u32[]{:S(2)}) %all-to-all-start.5) | async-done | bytes 544 | tf_op jit(solution)/shard_map/while/body/eval_jaxpr/all_to_all | solution.py:85
  420.3 8.0 %collective-permute-done.1 = f32[3,16,1024]{2,1,0:T(8,128)S(1)} collective-permute-done((f32[3,16,1024]{2,1,0:T(8,128)S(1)}, f32[3,16,1024]{2,1,0:T(8,128)S(1)}, u32[]{:S(2)}, u32[]{:S(2)}) %collective-permute-start.1) | collective-permute-done | bytes 196640 | tf_op jit(solution)/shard_map/while/body/eval_jaxpr/ppermute | solution.py:12
  (524 shorter events, 161.3 us)
Async XLA Ops:
  0.0 0.9 copy-start.2
  0.9 0.7 copy-start.3
  1.7 0.7 copy-start
  1.8 0.7 copy-start.1
  3.7 10.9 %all-to-all-start.2 = ((f32[8,8,2]{1,2,0:T(2,128)}), f32[8,8,2]{1,2,0:T(2,128)S(1)}, u32[]{:S(2)}, u32[]{:S(2)}) async-start(f32[8,8,2]{1,2,0:T(2,128)} %copy.117), calls=%async_computation.2 | async-start | bytes 16384 | tf_op jit(solution)/shard_map/while/body/eval_jaxpr/all_to_all | solution.py:77
  15.8 8.6 %all-to-all-start.3 = ((f32[8,8,2]{1,2,0:T(2,128)}), f32[8,8,2]{1,2,0:T(2,128)S(1)}, u32[]{:S(2)}, u32[]{:S(2)}) async-start(f32[8,8,2]{1,2,0:T(2,128)} %copy.119), calls=%async_computation.3 | async-start | bytes 16384 | tf_op jit(solution)/shard_map/while/body/eval_jaxpr/all_to_all | solution.py:85
  25.5 6.1 %collective-permute-start = (f32[3,16,1024]{2,1,0:T(8,128)S(1)}, f32[3,16,1024]{2,1,0:T(8,128)S(1)}, u32[]{:S(2)}, u32[]{:S(2)}) collective-permute-start(f32[3,16,1024]{2,1,0:T(8,128)S(1)} %get-tuple-element.1015), channel_id=1, source_target_pairs={{0,1},{1,2},{2,3},{4,5},{5,6},{6,7},{8,9},{9,10},{10,11},{12,13},{... | collective-permute-start | bytes 589832 | tf_op jit(solution)/shard_map/while/body/eval_jaxpr/ppermute | solution.py:12
  32.9 8.6 %all-to-all-start.2 = ((f32[8,8,2]{1,2,0:T(2,128)}), f32[8,8,2]{1,2,0:T(2,128)S(1)}, u32[]{:S(2)}, u32[]{:S(2)}) async-start(f32[8,8,2]{1,2,0:T(2,128)} %copy.117), calls=%async_computation.2 | async-start | bytes 16384 | tf_op jit(solution)/shard_map/while/body/eval_jaxpr/all_to_all | solution.py:77
  42.8 8.6 %all-to-all-start.3 = ((f32[8,8,2]{1,2,0:T(2,128)}), f32[8,8,2]{1,2,0:T(2,128)S(1)}, u32[]{:S(2)}, u32[]{:S(2)}) async-start(f32[8,8,2]{1,2,0:T(2,128)} %copy.119), calls=%async_computation.3 | async-start | bytes 16384 | tf_op jit(solution)/shard_map/while/body/eval_jaxpr/all_to_all | solution.py:85
  52.4 9.3 %collective-permute-start = (f32[3,16,1024]{2,1,0:T(8,128)S(1)}, f32[3,16,1024]{2,1,0:T(8,128)S(1)}, u32[]{:S(2)}, u32[]{:S(2)}) collective-permute-start(f32[3,16,1024]{2,1,0:T(8,128)S(1)} %get-tuple-element.1015), channel_id=1, source_target_pairs={{0,1},{1,2},{2,3},{4,5},{5,6},{6,7},{8,9},{9,10},{10,11},{12,13},{... | collective-permute-start | bytes 589832 | tf_op jit(solution)/shard_map/while/body/eval_jaxpr/ppermute | solution.py:12
  63.1 8.6 %all-to-all-start.2 = ((f32[8,8,2]{1,2,0:T(2,128)}), f32[8,8,2]{1,2,0:T(2,128)S(1)}, u32[]{:S(2)}, u32[]{:S(2)}) async-start(f32[8,8,2]{1,2,0:T(2,128)} %copy.117), calls=%async_computation.2 | async-start | bytes 16384 | tf_op jit(solution)/shard_map/while/body/eval_jaxpr/all_to_all | solution.py:77
  72.9 8.6 %all-to-all-start.3 = ((f32[8,8,2]{1,2,0:T(2,128)}), f32[8,8,2]{1,2,0:T(2,128)S(1)}, u32[]{:S(2)}, u32[]{:S(2)}) async-start(f32[8,8,2]{1,2,0:T(2,128)} %copy.119), calls=%async_computation.3 | async-start | bytes 16384 | tf_op jit(solution)/shard_map/while/body/eval_jaxpr/all_to_all | solution.py:85
  82.5 9.3 %collective-permute-start = (f32[3,16,1024]{2,1,0:T(8,128)S(1)}, f32[3,16,1024]{2,1,0:T(8,128)S(1)}, u32[]{:S(2)}, u32[]{:S(2)}) collective-permute-start(f32[3,16,1024]{2,1,0:T(8,128)S(1)} %get-tuple-element.1015), channel_id=1, source_target_pairs={{0,1},{1,2},{2,3},{4,5},{5,6},{6,7},{8,9},{9,10},{10,11},{12,13},{... | collective-permute-start | bytes 589832 | tf_op jit(solution)/shard_map/while/body/eval_jaxpr/ppermute | solution.py:12
  93.2 8.6 %all-to-all-start.2 = ((f32[8,8,2]{1,2,0:T(2,128)}), f32[8,8,2]{1,2,0:T(2,128)S(1)}, u32[]{:S(2)}, u32[]{:S(2)}) async-start(f32[8,8,2]{1,2,0:T(2,128)} %copy.117), calls=%async_computation.2 | async-start | bytes 16384 | tf_op jit(solution)/shard_map/while/body/eval_jaxpr/all_to_all | solution.py:77
  103.0 8.6 %all-to-all-start.3 = ((f32[8,8,2]{1,2,0:T(2,128)}), f32[8,8,2]{1,2,0:T(2,128)S(1)}, u32[]{:S(2)}, u32[]{:S(2)}) async-start(f32[8,8,2]{1,2,0:T(2,128)} %copy.119), calls=%async_computation.3 | async-start | bytes 16384 | tf_op jit(solution)/shard_map/while/body/eval_jaxpr/all_to_all | solution.py:85
  112.7 9.3 %collective-permute-start = (f32[3,16,1024]{2,1,0:T(8,128)S(1)}, f32[3,16,1024]{2,1,0:T(8,128)S(1)}, u32[]{:S(2)}, u32[]{:S(2)}) collective-permute-start(f32[3,16,1024]{2,1,0:T(8,128)S(1)} %get-tuple-element.1015), channel_id=1, source_target_pairs={{0,1},{1,2},{2,3},{4,5},{5,6},{6,7},{8,9},{9,10},{10,11},{12,13},{... | collective-permute-start | bytes 589832 | tf_op jit(solution)/shard_map/while/body/eval_jaxpr/ppermute | solution.py:12
  124.1 8.6 %all-to-all-start = ((f32[8,8,2]{1,2,0:T(2,128)}), f32[8,8,2]{1,2,0:T(2,128)S(1)}, u32[]{:S(2)}, u32[]{:S(2)}) async-start(f32[8,8,2]{1,2,0:T(2,128)} %copy.109), calls=%async_computation | async-start | bytes 16384 | tf_op jit(solution)/shard_map/while/body/eval_jaxpr/all_to_all | solution.py:77
  133.9 8.6 %all-to-all-start.1 = ((f32[8,8,2]{1,2,0:T(2,128)}), f32[8,8,2]{1,2,0:T(2,128)S(1)}, u32[]{:S(2)}, u32[]{:S(2)}) async-start(f32[8,8,2]{1,2,0:T(2,128)} %copy.111), calls=%async_computation.1 | async-start | bytes 16384 | tf_op jit(solution)/shard_map/while/body/eval_jaxpr/all_to_all | solution.py:85
  144.9 8.6 %all-to-all-start = ((f32[8,8,2]{1,2,0:T(2,128)}), f32[8,8,2]{1,2,0:T(2,128)S(1)}, u32[]{:S(2)}, u32[]{:S(2)}) async-start(f32[8,8,2]{1,2,0:T(2,128)} %copy.109), calls=%async_computation | async-start | bytes 16384 | tf_op jit(solution)/shard_map/while/body/eval_jaxpr/all_to_all | solution.py:77
  154.7 8.6 %all-to-all-start.1 = ((f32[8,8,2]{1,2,0:T(2,128)}), f32[8,8,2]{1,2,0:T(2,128)S(1)}, u32[]{:S(2)}, u32[]{:S(2)}) async-start(f32[8,8,2]{1,2,0:T(2,128)} %copy.111), calls=%async_computation.1 | async-start | bytes 16384 | tf_op jit(solution)/shard_map/while/body/eval_jaxpr/all_to_all | solution.py:85
  165.7 8.6 %all-to-all-start = ((f32[8,8,2]{1,2,0:T(2,128)}), f32[8,8,2]{1,2,0:T(2,128)S(1)}, u32[]{:S(2)}, u32[]{:S(2)}) async-start(f32[8,8,2]{1,2,0:T(2,128)} %copy.109), calls=%async_computation | async-start | bytes 16384 | tf_op jit(solution)/shard_map/while/body/eval_jaxpr/all_to_all | solution.py:77
  175.5 8.6 %all-to-all-start.1 = ((f32[8,8,2]{1,2,0:T(2,128)}), f32[8,8,2]{1,2,0:T(2,128)S(1)}, u32[]{:S(2)}, u32[]{:S(2)}) async-start(f32[8,8,2]{1,2,0:T(2,128)} %copy.111), calls=%async_computation.1 | async-start | bytes 16384 | tf_op jit(solution)/shard_map/while/body/eval_jaxpr/all_to_all | solution.py:85
  186.5 8.6 %all-to-all-start = ((f32[8,8,2]{1,2,0:T(2,128)}), f32[8,8,2]{1,2,0:T(2,128)S(1)}, u32[]{:S(2)}, u32[]{:S(2)}) async-start(f32[8,8,2]{1,2,0:T(2,128)} %copy.109), calls=%async_computation | async-start | bytes 16384 | tf_op jit(solution)/shard_map/while/body/eval_jaxpr/all_to_all | solution.py:77
  196.3 8.6 %all-to-all-start.1 = ((f32[8,8,2]{1,2,0:T(2,128)}), f32[8,8,2]{1,2,0:T(2,128)S(1)}, u32[]{:S(2)}, u32[]{:S(2)}) async-start(f32[8,8,2]{1,2,0:T(2,128)} %copy.111), calls=%async_computation.1 | async-start | bytes 16384 | tf_op jit(solution)/shard_map/while/body/eval_jaxpr/all_to_all | solution.py:85
  207.3 8.6 %all-to-all-start = ((f32[8,8,2]{1,2,0:T(2,128)}), f32[8,8,2]{1,2,0:T(2,128)S(1)}, u32[]{:S(2)}, u32[]{:S(2)}) async-start(f32[8,8,2]{1,2,0:T(2,128)} %copy.109), calls=%async_computation | async-start | bytes 16384 | tf_op jit(solution)/shard_map/while/body/eval_jaxpr/all_to_all | solution.py:77
  217.1 8.6 %all-to-all-start.1 = ((f32[8,8,2]{1,2,0:T(2,128)}), f32[8,8,2]{1,2,0:T(2,128)S(1)}, u32[]{:S(2)}, u32[]{:S(2)}) async-start(f32[8,8,2]{1,2,0:T(2,128)} %copy.111), calls=%async_computation.1 | async-start | bytes 16384 | tf_op jit(solution)/shard_map/while/body/eval_jaxpr/all_to_all | solution.py:85
  228.1 8.6 %all-to-all-start = ((f32[8,8,2]{1,2,0:T(2,128)}), f32[8,8,2]{1,2,0:T(2,128)S(1)}, u32[]{:S(2)}, u32[]{:S(2)}) async-start(f32[8,8,2]{1,2,0:T(2,128)} %copy.109), calls=%async_computation | async-start | bytes 16384 | tf_op jit(solution)/shard_map/while/body/eval_jaxpr/all_to_all | solution.py:77
  237.9 8.6 %all-to-all-start.1 = ((f32[8,8,2]{1,2,0:T(2,128)}), f32[8,8,2]{1,2,0:T(2,128)S(1)}, u32[]{:S(2)}, u32[]{:S(2)}) async-start(f32[8,8,2]{1,2,0:T(2,128)} %copy.111), calls=%async_computation.1 | async-start | bytes 16384 | tf_op jit(solution)/shard_map/while/body/eval_jaxpr/all_to_all | solution.py:85
  248.9 8.6 %all-to-all-start = ((f32[8,8,2]{1,2,0:T(2,128)}), f32[8,8,2]{1,2,0:T(2,128)S(1)}, u32[]{:S(2)}, u32[]{:S(2)}) async-start(f32[8,8,2]{1,2,0:T(2,128)} %copy.109), calls=%async_computation | async-start | bytes 16384 | tf_op jit(solution)/shard_map/while/body/eval_jaxpr/all_to_all | solution.py:77
  258.7 8.6 %all-to-all-start.1 = ((f32[8,8,2]{1,2,0:T(2,128)}), f32[8,8,2]{1,2,0:T(2,128)S(1)}, u32[]{:S(2)}, u32[]{:S(2)}) async-start(f32[8,8,2]{1,2,0:T(2,128)} %copy.111), calls=%async_computation.1 | async-start | bytes 16384 | tf_op jit(solution)/shard_map/while/body/eval_jaxpr/all_to_all | solution.py:85
  269.7 8.6 %all-to-all-start = ((f32[8,8,2]{1,2,0:T(2,128)}), f32[8,8,2]{1,2,0:T(2,128)S(1)}, u32[]{:S(2)}, u32[]{:S(2)}) async-start(f32[8,8,2]{1,2,0:T(2,128)} %copy.109), calls=%async_computation | async-start | bytes 16384 | tf_op jit(solution)/shard_map/while/body/eval_jaxpr/all_to_all | solution.py:77
  279.5 8.6 %all-to-all-start.1 = ((f32[8,8,2]{1,2,0:T(2,128)}), f32[8,8,2]{1,2,0:T(2,128)S(1)}, u32[]{:S(2)}, u32[]{:S(2)}) async-start(f32[8,8,2]{1,2,0:T(2,128)} %copy.111), calls=%async_computation.1 | async-start | bytes 16384 | tf_op jit(solution)/shard_map/while/body/eval_jaxpr/all_to_all | solution.py:85
  290.5 8.8 %all-to-all-start.4 = ((f32[8,8,2]{1,2,0:T(2,128)}), f32[8,8,2]{1,2,0:T(2,128)S(1)}, u32[]{:S(2)}, u32[]{:S(2)}) async-start(f32[8,8,2]{1,2,0:T(2,128)} %copy.125), calls=%async_computation.4 | async-start | bytes 16384 | tf_op jit(solution)/shard_map/while/body/eval_jaxpr/all_to_all | solution.py:77
  300.5 8.6 %all-to-all-start.5 = ((f32[8,8,2]{1,2,0:T(2,128)}), f32[8,8,2]{1,2,0:T(2,128)S(1)}, u32[]{:S(2)}, u32[]{:S(2)}) async-start(f32[8,8,2]{1,2,0:T(2,128)} %copy.127), calls=%async_computation.5 | async-start | bytes 16384 | tf_op jit(solution)/shard_map/while/body/eval_jaxpr/all_to_all | solution.py:85
  310.2 27.5 %collective-permute-start.1 = (f32[3,16,1024]{2,1,0:T(8,128)S(1)}, f32[3,16,1024]{2,1,0:T(8,128)S(1)}, u32[]{:S(2)}, u32[]{:S(2)}) collective-permute-start(f32[3,16,1024]{2,1,0:T(8,128)S(1)} %get-tuple-element.1048), channel_id=1, source_target_pairs={{0,1},{1,2},{2,3},{4,5},{5,6},{6,7},{8,9},{9,10},{10,11},{12,13},{... | collective-permute-start | bytes 589832 | tf_op jit(solution)/shard_map/while/body/eval_jaxpr/ppermute | solution.py:12
  339.1 8.6 %all-to-all-start.4 = ((f32[8,8,2]{1,2,0:T(2,128)}), f32[8,8,2]{1,2,0:T(2,128)S(1)}, u32[]{:S(2)}, u32[]{:S(2)}) async-start(f32[8,8,2]{1,2,0:T(2,128)} %copy.125), calls=%async_computation.4 | async-start | bytes 16384 | tf_op jit(solution)/shard_map/while/body/eval_jaxpr/all_to_all | solution.py:77
  348.9 8.6 %all-to-all-start.5 = ((f32[8,8,2]{1,2,0:T(2,128)}), f32[8,8,2]{1,2,0:T(2,128)S(1)}, u32[]{:S(2)}, u32[]{:S(2)}) async-start(f32[8,8,2]{1,2,0:T(2,128)} %copy.127), calls=%async_computation.5 | async-start | bytes 16384 | tf_op jit(solution)/shard_map/while/body/eval_jaxpr/all_to_all | solution.py:85
  358.6 9.3 %collective-permute-start.1 = (f32[3,16,1024]{2,1,0:T(8,128)S(1)}, f32[3,16,1024]{2,1,0:T(8,128)S(1)}, u32[]{:S(2)}, u32[]{:S(2)}) collective-permute-start(f32[3,16,1024]{2,1,0:T(8,128)S(1)} %get-tuple-element.1048), channel_id=1, source_target_pairs={{0,1},{1,2},{2,3},{4,5},{5,6},{6,7},{8,9},{9,10},{10,11},{12,13},{... | collective-permute-start | bytes 589832 | tf_op jit(solution)/shard_map/while/body/eval_jaxpr/ppermute | solution.py:12
  369.3 8.6 %all-to-all-start.4 = ((f32[8,8,2]{1,2,0:T(2,128)}), f32[8,8,2]{1,2,0:T(2,128)S(1)}, u32[]{:S(2)}, u32[]{:S(2)}) async-start(f32[8,8,2]{1,2,0:T(2,128)} %copy.125), calls=%async_computation.4 | async-start | bytes 16384 | tf_op jit(solution)/shard_map/while/body/eval_jaxpr/all_to_all | solution.py:77
  379.1 8.6 %all-to-all-start.5 = ((f32[8,8,2]{1,2,0:T(2,128)}), f32[8,8,2]{1,2,0:T(2,128)S(1)}, u32[]{:S(2)}, u32[]{:S(2)}) async-start(f32[8,8,2]{1,2,0:T(2,128)} %copy.127), calls=%async_computation.5 | async-start | bytes 16384 | tf_op jit(solution)/shard_map/while/body/eval_jaxpr/all_to_all | solution.py:85
  388.8 9.3 %collective-permute-start.1 = (f32[3,16,1024]{2,1,0:T(8,128)S(1)}, f32[3,16,1024]{2,1,0:T(8,128)S(1)}, u32[]{:S(2)}, u32[]{:S(2)}) collective-permute-start(f32[3,16,1024]{2,1,0:T(8,128)S(1)} %get-tuple-element.1048), channel_id=1, source_target_pairs={{0,1},{1,2},{2,3},{4,5},{5,6},{6,7},{8,9},{9,10},{10,11},{12,13},{... | collective-permute-start | bytes 589832 | tf_op jit(solution)/shard_map/while/body/eval_jaxpr/ppermute | solution.py:12
  399.5 8.6 %all-to-all-start.4 = ((f32[8,8,2]{1,2,0:T(2,128)}), f32[8,8,2]{1,2,0:T(2,128)S(1)}, u32[]{:S(2)}, u32[]{:S(2)}) async-start(f32[8,8,2]{1,2,0:T(2,128)} %copy.125), calls=%async_computation.4 | async-start | bytes 16384 | tf_op jit(solution)/shard_map/while/body/eval_jaxpr/all_to_all | solution.py:77
  409.3 8.6 %all-to-all-start.5 = ((f32[8,8,2]{1,2,0:T(2,128)}), f32[8,8,2]{1,2,0:T(2,128)S(1)}, u32[]{:S(2)}, u32[]{:S(2)}) async-start(f32[8,8,2]{1,2,0:T(2,128)} %copy.127), calls=%async_computation.5 | async-start | bytes 16384 | tf_op jit(solution)/shard_map/while/body/eval_jaxpr/all_to_all | solution.py:85
  419.0 9.3 %collective-permute-start.1 = (f32[3,16,1024]{2,1,0:T(8,128)S(1)}, f32[3,16,1024]{2,1,0:T(8,128)S(1)}, u32[]{:S(2)}, u32[]{:S(2)}) collective-permute-start(f32[3,16,1024]{2,1,0:T(8,128)S(1)} %get-tuple-element.1048), channel_id=1, source_target_pairs={{0,1},{1,2},{2,3},{4,5},{5,6},{6,7},{8,9},{9,10},{10,11},{12,13},{... | collective-permute-start | bytes 589832 | tf_op jit(solution)/shard_map/while/body/eval_jaxpr/ppermute | solution.py:12
where the time goes:
time: 435 us; the launch traced here: 429 us
  waiting for transfers between devices  241 us (55%)
  starting transfers between devices  119 us (27%)
  local copies, waits for them, and re-layouts  35.7 us (8%)
  other arithmetic  14.3 us (3%)
  matrix products  10.9 us (3%)
  loops' own time  6.73 us (2%)
    all_to_all x16, waiting for transfers between devices, attach_nodes(): lax.all_to_all(outbound.reshape(parts, slot_count, 2), 'net', split_axis=...  83.1 us
    all_to_all x16, waiting for transfers between devices, attach_nodes(): lax.all_to_all(reply, 'net', split_axis=0, concat_axis=0, tiled=True)  79.4 us
    ppermute x8, waiting for transfers between devices, passed_along(): lax.ppermute(value, axis, [(source, source + steps) for source in range(l...  78.9 us
    all_to_all x16, starting transfers between devices, attach_nodes(): lax.all_to_all(outbound.reshape(parts, slot_count, 2), 'net', split_axis=...  55.5 us
    all_to_all x16, starting transfers between devices, attach_nodes(): lax.all_to_all(reply, 'net', split_axis=0, concat_axis=0, tiled=True)  53.3 us
    another operation x48, local copies, waits for them, and re-layouts, attach_nodes(): jnp.stack([2.0 * slot_means[:, 0] - inbound[:, 0], slot_means[:, 1]], 1)  12.4 us
    reshape x32, local copies, waits for them, and re-layouts, attach_nodes(): outbound.reshape(parts, slot_count, 2)  11.5 us
    ppermute x8, starting transfers between devices, passed_along(): lax.ppermute(value, axis, [(source, source + steps) for source in range(l...  10.3 us
  transfers between devices with their start and end apart: 40, of which 40 were waited for; matrix products, arithmetic and copies ran while one was open for 0% of the time, Pallas kernels for 0%

commit v1 on v0

v1 whole, which is shorter than its diff:
```python
import functools

import jax
import jax.numpy as jnp
from jax import lax
from jax.experimental import pallas as pl
from jax.experimental.pallas import tpu as pltpu
from jax.sharding import PartitionSpec as P

STEPS_MAX = 8
STRIP = 16
LANES = 128
TABLE = 6 * STRIP
DRAG = TABLE + 8
GROUND = TABLE + 9
CODE_LEFT = TABLE + 10
CODE_RIGHT = TABLE + 11
MESH = pl.DeviceIdType.MESH


def roll(x, shift, axis):
    size = x.shape[axis]
    shift = shift % size
    return x if shift == 0 else pltpu.roll(x, shift, axis)


def column(row):
    pipes = row.shape[1]
    here = lax.broadcasted_iota(jnp.int32, (pipes, pipes), 0)
    there = lax.broadcasted_iota(jnp.int32, (pipes, pipes), 1)
    return jnp.sum(jnp.where(here == there, row, 0.0), axis=1, keepdims=True)


def gather_kernel(parts, slabs, x_ref, drag_ref, ground_ref, send_ref, recv_ref, steps_ref,
                  all_ref, count_ref, send_sem, recv_sem, step_send_sem, step_recv_sem):
    me = lax.axis_index("net")
    slab = lax.axis_index("tm")
    pipes = x_ref.shape[1]
    cells = x_ref.shape[2]
    slots = send_ref.shape[2]
    barrier = pltpu.get_barrier_semaphore()
    for off in range(1, parts):
        pl.semaphore_signal(barrier, inc=1, device_id={"net": lax.rem(me + off, parts)},
                            device_id_type=MESH)
    for off in range(1, slabs):
        pl.semaphore_signal(barrier, inc=1, device_id={"tm": lax.rem(slab + off, slabs)},
                            device_id_type=MESH)

    lane = lax.broadcasted_iota(jnp.int32, (pipes, LANES), 1)
    block = jnp.zeros((pipes, LANES), jnp.float32)
    for f in range(3):
        base = 2 * STRIP * f
        left = roll(x_ref[f, :, 0:LANES], base, 1)
        right = roll(x_ref[f, :, cells - LANES:cells], base + 2 * STRIP - LANES, 1)
        block = jnp.where((lane >= base) & (lane < base + STRIP), left, block)
        block = jnp.where((lane >= base + STRIP) & (lane < base + 2 * STRIP), right, block)
    pipe = lax.broadcasted_iota(jnp.int32, (pipes, slots), 0)
    slot = lax.broadcasted_iota(jnp.int32, (pipes, slots), 1) + (me // pipes) * slots
    code_left = jnp.zeros((pipes, slots), jnp.int32)
    code_right = jnp.zeros((pipes, slots), jnp.int32)
    for d in range(parts):
        listed = send_ref[0, d:d + 1, :]
        code_left = jnp.where(listed == pipe, slot + 8 * d, code_left)
        code_right = jnp.where(listed == pipe + pipes, slot + 8 * d, code_right)
    code_left = jnp.sum(code_left.astype(jnp.float32), axis=1, keepdims=True)
    code_right = jnp.sum(code_right.astype(jnp.float32), axis=1, keepdims=True)
    for at, value in ((DRAG, column(drag_ref[...].reshape(1, pipes))),
                      (GROUND, column(ground_ref[...].reshape(1, pipes))),
                      (CODE_LEFT, code_left), (CODE_RIGHT, code_right)):
        block = jnp.where(lane == at, value, block)
    mine = pl.ds(pl.multiple_of(me * pipes, pipes), pipes)
    all_ref[mine, :] = block
    for g in range(-(-parts // pipes)):
        rows = min(pipes, parts - g * pipes)
        all_ref[pl.ds(pl.multiple_of(me * pipes, pipes), rows),
                TABLE + g * slots:TABLE + (g + 1) * slots] = (
            recv_ref[0, g * pipes:g * pipes + rows, :].astype(jnp.float32))
    count_ref[slab] = jnp.full((8, LANES), steps_ref[0], jnp.int32)

    pl.semaphore_wait(barrier, parts - 1 + slabs - 1)
    copies = []
    for off in range(1, slabs):
        copies.append(pltpu.make_async_remote_copy(
            src_ref=count_ref.at[slab], dst_ref=count_ref.at[slab],
            send_sem=step_send_sem.at[off], recv_sem=step_recv_sem.at[off],
            device_id={"tm": lax.rem(slab + off, slabs)}, device_id_type=MESH))
    for off in range(1, parts):
        copies.append(pltpu.make_async_remote_copy(
            src_ref=all_ref.at[mine], dst_ref=all_ref.at[mine],
            send_sem=send_sem.at[off], recv_sem=recv_sem.at[off],
            device_id={"net": lax.rem(me + off, parts)}, device_id_type=MESH))
    for copy in copies:
        copy.start()
    for copy in copies:
        copy.wait()


def coarse_step(state, drag, cool, before, after, z=None):
    p, q, t = state
    zl, zr, tl, tr = (None,) * 4 if z is None else z
    a = before(p + q, zl)
    b = after(p - q, zr)
    return finish(a, b, q, t, 1.0, drag, cool, before, after, tl, tr)


def fine_step(state, h, drag, cool, before, after, z=None):
    p, q, t = state
    zl, zr, tl, tr = (None,) * 4 if z is None else z
    a = p + q
    b = p - q
    a = a - h * (a - before(a, zl))
    b = b - h * (b - after(b, zr))
    return finish(a, b, q, t, h, drag, cool, before, after, tl, tr)


def finish(a, b, q, t, h, drag, cool, before, after, tl, tr):
    r = 0.5 * (a - b)
    u = q / (1.0 + jnp.abs(q))
    flux = r / (1.0 + drag * jnp.abs(r))
    gain = jnp.maximum(u, 0.0) * (t - before(t, tl)) + jnp.minimum(u, 0.0) * (after(t, tr) - t)
    return 0.5 * (a + b), flux, (t - h * gain) * cool


def solve_kernel(parts, slabs, depth, x_ref, all_ref, steps_ref, out_ref,
                 deep_ref, u_ref, s_ref, v_ref, adj_ref, inv_ref, iu_ref, iv_ref, back_ref):
    me = lax.axis_index("net")
    slab = lax.axis_index("tm")
    pipes = x_ref.shape[1]
    cells = x_ref.shape[2]
    total = parts * pipes
    junctions = pipes // 2
    reach = slabs + STEPS_MAX - 1
    extra = depth - STRIP
    f32, bf16, i32 = jnp.float32, jnp.bfloat16, jnp.int32
    mine = pl.ds(pl.multiple_of(me * pipes, pipes), pipes)

    lane = lax.broadcasted_iota(i32, (pipes, LANES), 1)
    block = jnp.zeros((pipes, LANES), f32)
    for f in range(3):
        base = 2 * extra * f
        left = roll(x_ref[f, :, 0:LANES], base - STRIP, 1)
        right = roll(x_ref[f, :, cells - LANES:cells], base + extra - (LANES - depth), 1)
        block = jnp.where((lane >= base) & (lane < base + extra), left, block)
        block = jnp.where((lane >= base + extra) & (lane < base + 2 * extra), right, block)
    deep_ref[...] = jnp.zeros_like(deep_ref)
    deep_ref[mine, :] = block
    deep = deep_ref[...].T
    shallow = all_ref[...].T
    for f in range(3):
        base = 2 * STRIP * f
        near = 2 * extra * f
        s_ref[0, f, 0:STRIP, :] = shallow[base:base + STRIP]
        s_ref[0, f, STRIP:depth, :] = deep[near:near + extra]
        s_ref[0, f, depth:depth + extra, :] = deep[near + extra:near + 2 * extra]
        s_ref[0, f, depth + extra:2 * depth, :] = shallow[base + STRIP:base + 2 * STRIP]
    u_ref[0] = s_ref[0]
    v_ref[...] = s_ref[0]
    drag = shallow[DRAG:DRAG + 1]
    ground = shallow[GROUND:GROUND + 1]

    source = lax.broadcasted_iota(i32, (total, total), 0)
    target = lax.broadcasted_iota(i32, (total, total), 1)
    spread = ((source % pipes) == ((target // pipes) % pipes)).astype(f32).astype(bf16)
    table = shallow[TABLE:TABLE + 8]
    owner_of = lax.broadcasted_iota(i32, (8, total), 1) // pipes
    rows = jnp.concatenate([jnp.where(owner_of == d, table, 0.0) for d in range(parts)], 0)
    known = jnp.dot(rows.astype(bf16), spread, preferred_element_type=f32)
    place = lax.broadcasted_iota(i32, (8 * parts, total), 0)
    known = known + (junctions * (place // 8)).astype(f32)
    names = []
    for at in (CODE_LEFT, CODE_RIGHT):
        hit = place.astype(f32) == shallow[at:at + 1]
        names.append(jnp.sum(jnp.where(hit, known, 0.0), axis=0, keepdims=True))
    name = jnp.concatenate(names, 1)
    number = lax.broadcasted_iota(i32, (parts * junctions, 2 * total), 0).astype(f32)
    member = (number == name).astype(f32).astype(bf16)
    meets = lax.dot_general(member, member, (((0,), (0,)), ((), ())), preferred_element_type=f32)
    adj_ref[...] = meets.astype(bf16)
    inv_ref[...] = 1.0 / jnp.sum(meets, axis=0, keepdims=True)

    last = 2 * depth - 1
    row_at = lax.broadcasted_iota(i32, (2 * depth, total), 0)

    def before(x, z):
        return jnp.where(row_at == 0, z, roll(x, 1, 0))

    def after(x, z):
        return jnp.where(row_at == last, z, roll(x, -1, 0))

    def couple(states):
        count = len(states)
        height = -(-2 * count // 8) * 8
        at = lax.broadcasted_iota(i32, (height, 2 * total), 0)
        packed = jnp.zeros((height, 2 * total), f32)
        waves = []
        for n, (p, q, t) in enumerate(states):
            wave = jnp.concatenate(
                [p[0:1] - q[0:1], p[last:last + 1] + q[last:last + 1]], 1)
            waves.append(wave)
            warmth = jnp.concatenate([t[0:1], t[last:last + 1]], 1)
            packed = jnp.where(at == 2 * n, wave, packed)
            packed = jnp.where(at == 2 * n + 1, warmth, packed)
        high = packed.astype(bf16)
        rest = packed - high.astype(f32)
        mid = rest.astype(bf16)
        low = (rest - mid.astype(f32)).astype(bf16)
        adj = adj_ref[...]
        sums = (jnp.dot(low, adj, preferred_element_type=f32)
                + jnp.dot(mid, adj, preferred_element_type=f32)
                + jnp.dot(high, adj, preferred_element_type=f32))
        means = sums * inv_ref[...]
        ghosts = []
        for n in range(count):
            z = 2.0 * means[2 * n:2 * n + 1] - waves[n]
            th = means[2 * n + 1:2 * n + 2]
            ghosts.append((z[:, :total], z[:, total:], th[:, :total], th[:, total:]))
        return ghosts

    cool_one = 1.0 / (1.0 + ground)

    def coarse_strip(state):
        return coarse_step(state, drag, cool_one, before, after, couple([state])[0])

    def chain(n, carry):
        state = tuple(u_ref[n, f] for f in range(3))
        state = coarse_strip(state)
        for f in range(3):
            u_ref[n + 1, f] = state[f]
        return carry

    lax.fori_loop(0, slabs, chain, 0)
    for n in range(1, slabs):
        s_ref[n] = u_ref[n]
    hs, drags, cools = [], [], []
    for n in range(slabs):
        h = 1.0 / (jnp.zeros((1, total), f32) + steps_ref[n, 0, 0].astype(f32))
        hs.append(h)
        drags.append(h * drag)
        cools.append(1.0 / (1.0 + h * ground))

    def fine(m, carry):
        states = [tuple(s_ref[n, f] for f in range(3)) for n in range(slabs)]
        ghosts = couple(states)
        for n in range(slabs):
            @pl.when(m < steps_ref[n, 0, 0])
            def _():
                new = fine_step(states[n], hs[n], drags[n], cools[n], before, after, ghosts[n])
                for f in range(3):
                    s_ref[n, f] = new[f]
        return carry

    lax.fori_loop(0, STEPS_MAX, fine, 0)

    def correct(n, carry):
        state = coarse_strip(tuple(v_ref[f] for f in range(3)))
        for f in range(3):
            v_ref[f] = state[f] + (s_ref[n, f] - u_ref[n + 1, f])
        return carry

    lax.fori_loop(0, slab + 1, correct, 0)
    pieces = []
    for f in range(3):
        pieces.append(v_ref[f, 0:STRIP, :])
        pieces.append(v_ref[f, 2 * depth - STRIP:2 * depth, :])
    pieces.append(jnp.zeros((LANES - TABLE, total), f32))
    back_ref[...] = jnp.concatenate(pieces, 0).T

    for half in range(pipes // 8):
        span = pl.ds(half * 8, 8)
        own = pl.ds(pl.multiple_of(me * pipes + half * 8, 8), 8)
        params = all_ref[own, :]
        drag_c = jnp.broadcast_to(params[:, DRAG:DRAG + 1], (8, LANES))[:, 0:1]
        ground_c = params[:, GROUND:GROUND + 1]
        cool_c = 1.0 / (1.0 + ground_c)

        def left_of(x, z):
            return roll(x, 1, 1)

        def right_of(x, z):
            return roll(x, -1, 1)

        for f in range(3):
            iu_ref[f] = x_ref[f, span, :]
            iv_ref[f] = x_ref[f, span, :]

        def inner(n, carry):
            start = tuple(iu_ref[f] for f in range(3))
            count = steps_ref[n, 0, 0]
            h = 1.0 / (jnp.zeros((8, 1), f32) + count.astype(f32))
            drag_h = h * drag_c
            cool_h = 1.0 / (1.0 + h * ground_c)
            end = lax.fori_loop(
                0, count,
                lambda m, s: fine_step(s, h, drag_h, cool_h, left_of, right_of), start)
            guess = coarse_step(start, drag_c, cool_c, left_of, right_of)
            value = coarse_step(tuple(iv_ref[f] for f in range(3)), drag_c, cool_c,
                                left_of, right_of)
            for f in range(3):
                iu_ref[f] = guess[f]
                iv_ref[f] = value[f] + (end[f] - guess[f])
            return carry

        lax.fori_loop(0, slab + 1, inner, 0)
        ends = back_ref[own, :]
        lane8 = lax.broadcasted_iota(i32, (8, LANES), 1)
        for f in range(3):
            base = 2 * STRIP * f
            out_ref[0, f, span, :] = iv_ref[f]
            out_ref[0, f, span, 0:LANES] = jnp.where(
                lane8 < reach, roll(ends, -base, 1), iv_ref[f, :, 0:LANES])
            out_ref[0, f, span, cells - LANES:cells] = jnp.where(
                lane8 >= LANES - reach, roll(ends, LANES - 2 * STRIP - base, 1),
                iv_ref[f, :, cells - LANES:cells])


def body(parts, slabs, initial, wall_drag_factor, ground_exchange_rate, send_ends, recv_junction,
         slab_steps):
    pipes, cells = initial.shape[1:]
    total = parts * pipes
    depth = -(-2 * (slabs + STEPS_MAX - 1) // 8) * 8
    vmem = pl.BlockSpec(memory_space=pltpu.VMEM)
    smem = pl.BlockSpec(memory_space=pltpu.SMEM)
    gathered, counts = pl.pallas_call(
        functools.partial(gather_kernel, parts, slabs),
        out_shape=(jax.ShapeDtypeStruct((total, LANES), jnp.float32),
                   jax.ShapeDtypeStruct((slabs, 8, LANES), jnp.int32)),
        in_specs=[vmem] * 5 + [smem],
        out_specs=(vmem, vmem),
        scratch_shapes=[pltpu.SemaphoreType.DMA((parts,)), pltpu.SemaphoreType.DMA((parts,)),
                        pltpu.SemaphoreType.DMA((slabs,)), pltpu.SemaphoreType.DMA((slabs,))],
        compiler_params=pltpu.CompilerParams(collective_id=0, has_side_effects=True),
        name="gather_ends",
    )(initial, wall_drag_factor, ground_exchange_rate, send_ends, recv_junction, slab_steps)
    return pl.pallas_call(
        functools.partial(solve_kernel, parts, slabs, depth),
        out_shape=jax.ShapeDtypeStruct((1, 3, pipes, cells), jnp.float32),
        in_specs=[vmem, vmem, smem],
        out_specs=vmem,
        scratch_shapes=[
            pltpu.VMEM((total, LANES), jnp.float32),
            pltpu.VMEM((slabs + 1, 3, 2 * depth, total), jnp.float32),
            pltpu.VMEM((slabs, 3, 2 * depth, total), jnp.float32),
            pltpu.VMEM((3, 2 * depth, total), jnp.float32),
            pltpu.VMEM((2 * total, 2 * total), jnp.bfloat16),
            pltpu.VMEM((1, 2 * total), jnp.float32),
            pltpu.VMEM((3, 8, cells), jnp.float32),
            pltpu.VMEM((3, 8, cells), jnp.float32),
            pltpu.VMEM((total, LANES), jnp.float32),
        ],
        name="solve",
    )(initial, gathered, counts)


def solution(mesh):
    return jax.shard_map(
        functools.partial(body, mesh.shape["net"], mesh.shape["tm"]),
        mesh=mesh,
        in_specs=(
            P(None, "net", None),
            P("net"),
            P("net"),
            P("net", None, None),
            P("net", None, None),
            P("tm"),
        ),
        out_specs=P("tm", None, "net", None),
        check_vma=False,
    )
```

time: 435 us -> 23.6 us (0.05); the launches traced: 429 us -> 23.7 us
  waiting for transfers between devices: 241 us -> 0 us
  starting transfers between devices: 119 us -> 0 us
  local copies, waits for them, and re-layouts: 35.7 us -> 0 us
  Pallas kernels: 0 us -> 23.1 us
  other arithmetic: 14.3 us -> 0 us
  matrix products: 10.9 us -> 0 us
  loops' own time: 6.73 us -> 0 us
    all_to_all x32 -> x0, waiting for transfers between devices: 163 us -> none  [the longest x16 83.1 us: attach_nodes(): lax.all_to_all(outbound.reshape(parts, slot_count, 2), 'net', split_axis=...]
    all_to_all x32 -> x0, starting transfers between devices: 109 us -> none  [the longest x16 55.5 us: attach_nodes(): lax.all_to_all(outbound.reshape(parts, slot_count, 2), 'net', split_axis=...]
    ppermute x8 -> x0, waiting for transfers between devices: 78.9 us -> none  [passed_along(): lax.ppermute(value, axis, [(source, source + steps) for source in range(l...]
    pallas_call x0 -> x2, Pallas kernels: none -> 23.1 us  [the longest x1 14.3 us: body(): pl.pallas_call(functools.partial(solve_kernel, parts, slabs, depth), out_...]
    reshape x64 -> x0, local copies, waits for them, and re-layouts: 14.2 us -> none  [the longest x32 11.5 us: attach_nodes(): outbound.reshape(parts, slot_count, 2)]
    another operation x48 -> x0, local copies, waits for them, and re-layouts: 12.4 us -> none  [attach_nodes(): jnp.stack([2.0 * slot_means[:, 0] - inbound[:, 0], slot_means[:, 1]], 1)]
    dot_general x64 -> x0, matrix products: 10.9 us -> none  [the longest x16 3.43 us: attach_nodes(): outbound = jnp.dot(send_onehot, local_entries, precision=highest)]
    ppermute x8 -> x0, starting transfers between devices: 10.3 us -> none  [passed_along(): lax.ppermute(value, axis, [(source, source + steps) for source in range(l...]
  transfers between devices with their start and end apart: 40 -> 0, of which waited for: 40 -> 0; matrix products, arithmetic and copies ran while one was open for 0% -> 0% of each run, Pallas kernels for 0% -> 0%
where the time goes in v1:
time: 23.6 us; the launch traced here: 23.7 us
  Pallas kernels  23.1 us (98%)
  between operations  0.66 us (3%)
    pallas_call x1, Pallas kernels, body(): pl.pallas_call(functools.partial(solve_kernel, parts, slabs, depth), out_...  14.3 us
    pallas_call x1, Pallas kernels, body(): pl.pallas_call(functools.partial(gather_kernel, parts, slabs), out_shape=...  8.78 us

profile of v1, /device:TPU:5, one launch (start us, length us, event | category | flops | bytes accessed | tf_op | source)
XLA Modules:
  0.0 23.7 jit_solution(7183725952668725609)
XLA Ops:
  0.7 8.8 %gather_ends.1 = (f32[128,128]{1,0:T(8,128)}, s32[4,8,128]{2,1,0:T(8,128)}) custom-call(f32[3,16,1024]{2,1,0:T(8,128)} %x_ref.3, f32[16]{0:T(128)} %drag_ref.1, f32[16]{0:T(128)} %ground_ref.1, s32[1,8,8]{2,1,0:T(8,128)} %send_ref.1, s32[1,8,8]{2,1,0:T(8,128)} %recv_ref.1, s32[1]{0:T(128)S(6)} %copy.7.steps_ref), custom_call_target="tpu_custom_call" | custom-call | tf_op jit(solution)/shard_map/gather_ends/pallas_call | solution.py:323
  9.4 14.3 %solve.1 = f32[1,3,16,1024]{3,2,1,0:T(8,128)} custom-call(f32[3,16,1024]{2,1,0:T(8,128)} %x_ref.3, f32[128,128]{1,0:T(8,128)} %get-tuple-element.7.all_ref, s32[4,8,128]{2,1,0:T(8,128)} %get-tuple-element.8.steps_ref), custom_call_target="tpu_custom_call" | custom-call | tf_op jit(solution)/shard_map/solve/pallas_call | solution.py:334

commit v2 on v1

--- a/solution.py
+++ b/solution.py
@@ -8,6 +8,7 @@
 from jax.sharding import PartitionSpec as P
 
 STEPS_MAX = 8
+STEPS_MIN = 4
 STRIP = 16
 LANES = 128
 TABLE = 6 * STRIP
@@ -31,8 +32,8 @@
     return jnp.sum(jnp.where(here == there, row, 0.0), axis=1, keepdims=True)
 
 
-def gather_kernel(parts, slabs, x_ref, drag_ref, ground_ref, send_ref, recv_ref, steps_ref,
-                  all_ref, count_ref, send_sem, recv_sem, step_send_sem, step_recv_sem):
+def gather_kernel(parts, slabs, depth, x_ref, drag_ref, ground_ref, send_ref, recv_ref, steps_ref,
+                  all_ref, count_ref, deep_ref, mid_ref, iu_ref, iv_ref, send_sem, recv_sem, step_send_sem, step_recv_sem):
     me = lax.axis_index("net")
     slab = lax.axis_index("tm")
     pipes = x_ref.shape[1]
@@ -91,7 +92,64 @@
             device_id={"net": lax.rem(me + off, parts)}, device_id_type=MESH))
     for copy in copies:
         copy.start()
-    for copy in copies:
+
+    extra = depth - STRIP
+    block = jnp.zeros((pipes, LANES), jnp.float32)
+    for f in range(3):
+        base = 2 * extra * f
+        left = roll(x_ref[f, :, 0:LANES], base - STRIP, 1)
+        right = roll(x_ref[f, :, cells - LANES:cells], base + extra - (LANES - depth), 1)
+        block = jnp.where((lane >= base) & (lane < base + extra), left, block)
+        block = jnp.where((lane >= base + extra) & (lane < base + 2 * extra), right, block)
+    deep_ref[...] = block
+    for copy in copies[:slabs - 1]:
+        copy.wait()
+
+    def left_of(x, z):
+        return roll(x, 1, 1)
+
+    def right_of(x, z):
+        return roll(x, -1, 1)
+
+    for half in range(pipes // 8):
+        span = pl.ds(half * 8, 8)
+        own = pl.ds(pl.multiple_of(me * pipes + half * 8, 8), 8)
+        params = all_ref[own, :]
+        drag_c = params[:, DRAG:DRAG + 1]
+        ground_c = params[:, GROUND:GROUND + 1]
+        cool_c = 1.0 / (1.0 + ground_c)
+        for f in range(3):
+            iu_ref[f] = x_ref[f, span, :]
+            iv_ref[f] = x_ref[f, span, :]
+
+        def inner(n, carry):
+            start = tuple(iu_ref[f] for f in range(3))
+            count = count_ref[n]
+            h = 1.0 / count[:, 0:1].astype(jnp.float32)
+            drag_h = h * drag_c
+            cool_h = 1.0 / (1.0 + h * ground_c)
+
+            def step(m, s):
+                return fine_step(s, h, drag_h, cool_h, left_of, right_of)
+
+            def maybe(m, s):
+                live = jnp.concatenate([m < count] * (cells // LANES), 1)
+                return tuple(jnp.where(live, a, b) for a, b in zip(step(m, s), s))
+
+            end = lax.fori_loop(0, STEPS_MIN, step, start)
+            end = lax.fori_loop(STEPS_MIN, STEPS_MAX, maybe, end)
+            guess = coarse_step(start, drag_c, cool_c, left_of, right_of)
+            value = coarse_step(tuple(iv_ref[f] for f in range(3)), drag_c, cool_c,
+                                left_of, right_of)
+            for f in range(3):
+                iu_ref[f] = guess[f]
+                iv_ref[f] = value[f] + (end[f] - guess[f])
+            return carry
+
+        lax.fori_loop(0, slab + 1, inner, 0)
+        for f in range(3):
+            mid_ref[0, f, span, :] = iv_ref[f]
+    for copy in copies[slabs - 1:]:
         copy.wait()
 
 
@@ -100,7 +158,7 @@
     zl, zr, tl, tr = (None,) * 4 if z is None else z
     a = before(p + q, zl)
     b = after(p - q, zr)
-    return finish(a, b, q, t, 1.0, drag, cool, before, after, tl, tr)
+    return finish(0.5 * (a + b), 0.5 * (a - b), q, t, None, drag, cool, before, after, tl, tr)
 
 
 def fine_step(state, h, drag, cool, before, after, z=None):
@@ -108,25 +166,30 @@
     zl, zr, tl, tr = (None,) * 4 if z is None else z
     a = p + q
     b = p - q
-    a = a - h * (a - before(a, zl))
-    b = b - h * (b - after(b, zr))
-    return finish(a, b, q, t, h, drag, cool, before, after, tl, tr)
-
-
-def finish(a, b, q, t, h, drag, cool, before, after, tl, tr):
-    r = 0.5 * (a - b)
-    u = q / (1.0 + jnp.abs(q))
-    flux = r / (1.0 + drag * jnp.abs(r))
+    da = a - before(a, zl)
+    db = b - after(b, zr)
+    half = 0.5 * h
+    return finish(p - half * (da + db), q - half * (da - db), q, t, h, drag, cool, before, after,
+                  tl, tr)
+
+
+def finish(p, r, q, t, h, drag, cool, before, after, tl, tr):
+    slow = 1.0 + jnp.abs(q)
+    dragged = 1.0 + drag * jnp.abs(r)
+    inverse = 1.0 / (slow * dragged)
+    u = q * (dragged * inverse)
     gain = jnp.maximum(u, 0.0) * (t - before(t, tl)) + jnp.minimum(u, 0.0) * (after(t, tr) - t)
-    return 0.5 * (a + b), flux, (t - h * gain) * cool
-
-
-def solve_kernel(parts, slabs, depth, x_ref, all_ref, steps_ref, out_ref,
-                 deep_ref, u_ref, s_ref, v_ref, adj_ref, inv_ref, iu_ref, iv_ref, back_ref):
+    if h is not None:
+        gain = h * gain
+    return p, r * (slow * inverse), (t - gain) * cool
+
+
+def solve_kernel(parts, slabs, depth, mid_ref, own_ref, all_ref, steps_ref, out_ref,
+                 deep_ref, u_ref, s_ref, v_ref, adj_ref, inv_ref, back_ref):
     me = lax.axis_index("net")
     slab = lax.axis_index("tm")
-    pipes = x_ref.shape[1]
-    cells = x_ref.shape[2]
+    pipes = mid_ref.shape[2]
+    cells = mid_ref.shape[3]
     total = parts * pipes
     junctions = pipes // 2
     reach = slabs + STEPS_MAX - 1
@@ -134,16 +197,8 @@
     f32, bf16, i32 = jnp.float32, jnp.bfloat16, jnp.int32
     mine = pl.ds(pl.multiple_of(me * pipes, pipes), pipes)
 
-    lane = lax.broadcasted_iota(i32, (pipes, LANES), 1)
-    block = jnp.zeros((pipes, LANES), f32)
-    for f in range(3):
-        base = 2 * extra * f
-        left = roll(x_ref[f, :, 0:LANES], base - STRIP, 1)
-        right = roll(x_ref[f, :, cells - LANES:cells], base + extra - (LANES - depth), 1)
-        block = jnp.where((lane >= base) & (lane < base + extra), left, block)
-        block = jnp.where((lane >= base + extra) & (lane < base + 2 * extra), right, block)
     deep_ref[...] = jnp.zeros_like(deep_ref)
-    deep_ref[mine, :] = block
+    deep_ref[mine, :] = own_ref[...]
     deep = deep_ref[...].T
     shallow = all_ref[...].T
     for f in range(3):
@@ -153,8 +208,6 @@
         s_ref[0, f, STRIP:depth, :] = deep[near:near + extra]
         s_ref[0, f, depth:depth + extra, :] = deep[near + extra:near + 2 * extra]
         s_ref[0, f, depth + extra:2 * depth, :] = shallow[base + STRIP:base + 2 * STRIP]
-    u_ref[0] = s_ref[0]
-    v_ref[...] = s_ref[0]
     drag = shallow[DRAG:DRAG + 1]
     ground = shallow[GROUND:GROUND + 1]
 
@@ -217,20 +270,6 @@
         return ghosts
 
     cool_one = 1.0 / (1.0 + ground)
-
-    def coarse_strip(state):
-        return coarse_step(state, drag, cool_one, before, after, couple([state])[0])
-
-    def chain(n, carry):
-        state = tuple(u_ref[n, f] for f in range(3))
-        state = coarse_strip(state)
-        for f in range(3):
-            u_ref[n + 1, f] = state[f]
-        return carry
-
-    lax.fori_loop(0, slabs, chain, 0)
-    for n in range(1, slabs):
-        s_ref[n] = u_ref[n]
     hs, drags, cools = [], [], []
     for n in range(slabs):
         h = 1.0 / (jnp.zeros((1, total), f32) + steps_ref[n, 0, 0].astype(f32))
@@ -238,79 +277,71 @@
         drags.append(h * drag)
         cools.append(1.0 / (1.0 + h * ground))
 
-    def fine(m, carry):
-        states = [tuple(s_ref[n, f] for f in range(3)) for n in range(slabs)]
+    def coarse(state, ghosts):
+        return coarse_step(state, drag, cool_one, before, after, ghosts)
+
+    def load(ref, n):
+        return tuple(ref[n, f] for f in range(3))
+
+    def store(ref, n, state):
+        for f in range(3):
+            ref[n, f] = state[f]
+
+    def advance(n, m, state, ghosts):
+        new = fine_step(state, hs[n], drags[n], cools[n], before, after, ghosts)
+        if isinstance(m, int) and m < STEPS_MIN:
+            return new
+        live = m < steps_ref[n, 0, 0]
+        return tuple(jnp.where(live, a, b) for a, b in zip(new, state))
+
+    for t in range(slabs):
+        states = [load(s_ref, n) for n in range(t + 1)]
+        ghosts = couple(states)
+        guess = coarse(states[t], ghosts[t])
+        store(u_ref, t, guess)
+        if t + 1 < slabs:
+            store(s_ref, t + 1, guess)
+        for n in range(t + 1):
+            store(s_ref, n, advance(n, t - n, states[n], ghosts[n]))
+
+    def stage(t, carry):
+        states = [load(s_ref, n) for n in range(slabs)]
         ghosts = couple(states)
         for n in range(slabs):
-            @pl.when(m < steps_ref[n, 0, 0])
-            def _():
-                new = fine_step(states[n], hs[n], drags[n], cools[n], before, after, ghosts[n])
-                for f in range(3):
-                    s_ref[n, f] = new[f]
+            store(s_ref, n, advance(n, t - n, states[n], ghosts[n]))
         return carry
 
-    lax.fori_loop(0, STEPS_MAX, fine, 0)
-
-    def correct(n, carry):
-        state = coarse_strip(tuple(v_ref[f] for f in range(3)))
-        for f in range(3):
-            v_ref[f] = state[f] + (s_ref[n, f] - u_ref[n + 1, f])
-        return carry
-
-    lax.fori_loop(0, slab + 1, correct, 0)
+    lax.fori_loop(slabs, STEPS_MAX, stage, 0)
+    value = load(s_ref, 0)
+    store(v_ref, 0, value)
+    for t in range(STEPS_MAX, STEPS_MAX + slabs - 1):
+        first = t - STEPS_MAX + 1
+        states = [load(s_ref, n) for n in range(first, slabs)]
+        ghosts = couple([value] + states)
+        guess = load(u_ref, first)
+        ends = [advance(n, t - n, states[n - first], ghosts[n - first + 1])
+                for n in range(first, slabs)]
+        for n in range(first + 1, slabs):
+            store(s_ref, n, ends[n - first])
+        value = tuple(g + (e - u) for g, e, u in zip(coarse(value, ghosts[0]), ends[0], guess))
+        store(v_ref, first, value)
     pieces = []
     for f in range(3):
-        pieces.append(v_ref[f, 0:STRIP, :])
-        pieces.append(v_ref[f, 2 * depth - STRIP:2 * depth, :])
+        pieces.append(v_ref[slab, f, 0:STRIP, :])
+        pieces.append(v_ref[slab, f, 2 * depth - STRIP:2 * depth, :])
     pieces.append(jnp.zeros((LANES - TABLE, total), f32))
     back_ref[...] = jnp.concatenate(pieces, 0).T
 
-    for half in range(pipes // 8):
-        span = pl.ds(half * 8, 8)
-        own = pl.ds(pl.multiple_of(me * pipes + half * 8, 8), 8)
-        params = all_ref[own, :]
-        drag_c = jnp.broadcast_to(params[:, DRAG:DRAG + 1], (8, LANES))[:, 0:1]
-        ground_c = params[:, GROUND:GROUND + 1]
-        cool_c = 1.0 / (1.0 + ground_c)
-
-        def left_of(x, z):
-            return roll(x, 1, 1)
-
-        def right_of(x, z):
-            return roll(x, -1, 1)
-
-        for f in range(3):
-            iu_ref[f] = x_ref[f, span, :]
-            iv_ref[f] = x_ref[f, span, :]
-
-        def inner(n, carry):
-            start = tuple(iu_ref[f] for f in range(3))
-            count = steps_ref[n, 0, 0]
-            h = 1.0 / (jnp.zeros((8, 1), f32) + count.astype(f32))
-            drag_h = h * drag_c
-            cool_h = 1.0 / (1.0 + h * ground_c)
-            end = lax.fori_loop(
-                0, count,
-                lambda m, s: fine_step(s, h, drag_h, cool_h, left_of, right_of), start)
-            guess = coarse_step(start, drag_c, cool_c, left_of, right_of)
-            value = coarse_step(tuple(iv_ref[f] for f in range(3)), drag_c, cool_c,
-                                left_of, right_of)
-            for f in range(3):
-                iu_ref[f] = guess[f]
-                iv_ref[f] = value[f] + (end[f] - guess[f])
-            return carry
-
-        lax.fori_loop(0, slab + 1, inner, 0)
-        ends = back_ref[own, :]
-        lane8 = lax.broadcasted_iota(i32, (8, LANES), 1)
-        for f in range(3):
-            base = 2 * STRIP * f
-            out_ref[0, f, span, :] = iv_ref[f]
-            out_ref[0, f, span, 0:LANES] = jnp.where(
-                lane8 < reach, roll(ends, -base, 1), iv_ref[f, :, 0:LANES])
-            out_ref[0, f, span, cells - LANES:cells] = jnp.where(
-                lane8 >= LANES - reach, roll(ends, LANES - 2 * STRIP - base, 1),
-                iv_ref[f, :, cells - LANES:cells])
+    ends = back_ref[mine, :]
+    lane = lax.broadcasted_iota(i32, (pipes, LANES), 1)
+    for f in range(3):
+        base = 2 * STRIP * f
+        out_ref[0, f, :, LANES:cells - LANES] = mid_ref[0, f, :, LANES:cells - LANES]
+        out_ref[0, f, :, 0:LANES] = jnp.where(
+            lane < reach, roll(ends, -base, 1), mid_ref[0, f, :, 0:LANES])
+        out_ref[0, f, :, cells - LANES:cells] = jnp.where(
+            lane >= LANES - reach, roll(ends, LANES - 2 * STRIP - base, 1),
+            mid_ref[0, f, :, cells - LANES:cells])
 
 
 def body(parts, slabs, initial, wall_drag_factor, ground_exchange_rate, send_ends, recv_junction,
@@ -320,13 +351,17 @@
     depth = -(-2 * (slabs + STEPS_MAX - 1) // 8) * 8
     vmem = pl.BlockSpec(memory_space=pltpu.VMEM)
     smem = pl.BlockSpec(memory_space=pltpu.SMEM)
-    gathered, counts = pl.pallas_call(
-        functools.partial(gather_kernel, parts, slabs),
+    gathered, counts, own, mid = pl.pallas_call(
+        functools.partial(gather_kernel, parts, slabs, depth),
         out_shape=(jax.ShapeDtypeStruct((total, LANES), jnp.float32),
-                   jax.ShapeDtypeStruct((slabs, 8, LANES), jnp.int32)),
+                   jax.ShapeDtypeStruct((slabs, 8, LANES), jnp.int32),
+                   jax.ShapeDtypeStruct((pipes, LANES), jnp.float32),
+                   jax.ShapeDtypeStruct((1, 3, pipes, cells), jnp.float32)),
         in_specs=[vmem] * 5 + [smem],
-        out_specs=(vmem, vmem),
-        scratch_shapes=[pltpu.SemaphoreType.DMA((parts,)), pltpu.SemaphoreType.DMA((parts,)),
+        out_specs=(vmem,) * 4,
+        scratch_shapes=[pltpu.VMEM((3, 8, cells), jnp.float32),
+                        pltpu.VMEM((3, 8, cells), jnp.float32),
+                        pltpu.SemaphoreType.DMA((parts,)), pltpu.SemaphoreType.DMA((parts,)),
                         pltpu.SemaphoreType.DMA((slabs,)), pltpu.SemaphoreType.DMA((slabs,))],
         compiler_params=pltpu.CompilerParams(collective_id=0, has_side_effects=True),
         name="gather_ends",
@@ -334,21 +369,19 @@
     return pl.pallas_call(
         functools.partial(solve_kernel, parts, slabs, depth),
         out_shape=jax.ShapeDtypeStruct((1, 3, pipes, cells), jnp.float32),
-        in_specs=[vmem, vmem, smem],
+        in_specs=[vmem, vmem, vmem, smem],
         out_specs=vmem,
         scratch_shapes=[
             pltpu.VMEM((total, LANES), jnp.float32),
-            pltpu.VMEM((slabs + 1, 3, 2 * depth, total), jnp.float32),
             pltpu.VMEM((slabs, 3, 2 * depth, total), jnp.float32),
-            pltpu.VMEM((3, 2 * depth, total), jnp.float32),
+            pltpu.VMEM((slabs, 3, 2 * depth, total), jnp.float32),
+            pltpu.VMEM((slabs, 3, 2 * depth, total), jnp.float32),
             pltpu.VMEM((2 * total, 2 * total), jnp.bfloat16),
             pltpu.VMEM((1, 2 * total), jnp.float32),
-            pltpu.VMEM((3, 8, cells), jnp.float32),
-            pltpu.VMEM((3, 8, cells), jnp.float32),
             pltpu.VMEM((total, LANES), jnp.float32),
         ],
         name="solve",
-    )(initial, gathered, counts)
+    )(mid, own, gathered, counts)
 
 
 def solution(mesh):

time: 23.6 us -> 24.7 us (1.047); the launches traced: 23.7 us -> 24.5 us
  Pallas kernels: 23.1 us -> 23.8 us
    pallas_call x1, Pallas kernels: 8.78 us -> 18.6 us  [body(): pl.pallas_call(functools.partial(gather_kernel, parts, slabs, depth), out...]
    pallas_call x1, Pallas kernels: 14.3 us -> 5.19 us  [body(): pl.pallas_call(functools.partial(solve_kernel, parts, slabs, depth), out_...]
where the time goes in v2:
time: 24.7 us; the launch traced here: 24.5 us
  Pallas kernels  23.8 us (96%)
  between operations  0.66 us (3%)
    pallas_call x1, Pallas kernels, body(): pl.pallas_call(functools.partial(gather_kernel, parts, slabs, depth), out...  18.6 us
    pallas_call x1, Pallas kernels, body(): pl.pallas_call(functools.partial(solve_kernel, parts, slabs, depth), out_...  5.19 us

profile of v2, /device:TPU:5, one launch (start us, length us, event | category | flops | bytes accessed | tf_op | source)
XLA Modules:
  0.0 24.5 jit_solution(1769878396430655413)
XLA Ops:
  0.7 18.6 %gather_ends.1 = (f32[128,128]{1,0:T(8,128)}, s32[4,8,128]{2,1,0:T(8,128)}, f32[16,128]{1,0:T(8,128)}, f32[1,3,16,1024]{3,2,1,0:T(8,128)}) custom-call(f32[3,16,1024]{2,1,0:T(8,128)} %x_ref.1, f32[16]{0:T(128)} %drag_ref.1, f32[16]{0:T(128)} %ground_ref.1, s32[1,8,8]{2,1,0:T(8,128)} %send_ref.1, s32[1,8,8]{2,1,0:T(8,128)} %recv_ref.1, s32[1]{0:T(128)S(6)} %copy.7.steps_ref), custom_call_target="tpu_custom_call" | custom-call | tf_op jit(solution)/shard_map/gather_ends/pallas_call | solution.py:354
  19.3 5.2 %solve.1 = f32[1,3,16,1024]{3,2,1,0:T(8,128)} custom-call(f32[1,3,16,1024]{3,2,1,0:T(8,128)} %get-tuple-element.9.mid_ref, f32[16,128]{1,0:T(8,128)} %get-tuple-element.10.own_ref, f32[128,128]{1,0:T(8,128)} %get-tuple-element.11.all_ref, s32[4,8,128]{2,1,0:T(8,128)} %get-tuple-element.12.steps_ref), custom_call_target="tpu_custom_call" | custom-call | tf_op jit(solution)/shard_map/solve/pallas_call | solution.py:369

commit v3 on v2

--- a/solution.py
+++ b/solution.py
@@ -12,6 +12,8 @@
 STRIP = 16
 LANES = 128
 TABLE = 6 * STRIP
+PAD = 8
+HALO = 16
 DRAG = TABLE + 8
 GROUND = TABLE + 9
 CODE_LEFT = TABLE + 10
@@ -32,8 +34,37 @@
     return jnp.sum(jnp.where(here == there, row, 0.0), axis=1, keepdims=True)
 
 
+def sweep(source, targets, rows, chunk, h, drag, cool, live=None):
+    for low in range(PAD, PAD + rows, chunk):
+        here, prior, coming = (pl.ds(low + off, chunk) for off in (0, -1, 1))
+        a, b, t = (source[f, here, :] for f in range(3))
+        a_prior, t_prior = source[0, prior, :], source[2, prior, :]
+        b_coming, t_coming = source[1, coming, :], source[2, coming, :]
+        q = 0.5 * (a - b)
+        if h is None:
+            ahead, back = a_prior, b_coming
+        else:
+            ahead, back = a - h * (a - a_prior), b - h * (b - b_coming)
+        p = 0.5 * (ahead + back)
+        r = 0.5 * (ahead - back)
+        slow = 1.0 + jnp.abs(q)
+        dragged = 1.0 + drag * jnp.abs(r)
+        inverse = 1.0 / (slow * dragged)
+        flux = r * (slow * inverse)
+        u = q * (dragged * inverse)
+        gain = jnp.maximum(u, 0.0) * (t - t_prior) + jnp.minimum(u, 0.0) * (t_coming - t)
+        if h is not None:
+            gain = h * gain
+        new = (p + flux, p - flux, (t - gain) * cool)
+        if live is not None:
+            new = tuple(jnp.where(live, x, y) for x, y in zip(new, (a, b, t)))
+        for target in targets:
+            for f in range(3):
+                target[f, here, :] = new[f]
+
+
 def gather_kernel(parts, slabs, depth, x_ref, drag_ref, ground_ref, send_ref, recv_ref, steps_ref,
-                  all_ref, count_ref, deep_ref, mid_ref, iu_ref, iv_ref, send_sem, recv_sem, step_send_sem, step_recv_sem):
+                  all_ref, count_ref, deep_ref, mid_ref, fold_ref, send_sem, recv_sem, step_send_sem, step_recv_sem):
     me = lax.axis_index("net")
     slab = lax.axis_index("tm")
     pipes = x_ref.shape[1]
@@ -78,6 +109,19 @@
             recv_ref[0, g * pipes:g * pipes + rows, :].astype(jnp.float32))
     count_ref[slab] = jnp.full((8, LANES), steps_ref[0], jnp.int32)
 
+    segments = cells // LANES
+    rows = LANES + 2 * HALO
+    fold_ref[:, :, 0:PAD, :] = jnp.zeros((5, 3, PAD, LANES), jnp.float32)
+    fold_ref[:, :, PAD + rows:, :] = jnp.zeros((5, 3, PAD, LANES), jnp.float32)
+    turned = [jnp.concatenate([x_ref[f, :, LANES * c:LANES * (c + 1)] for c in range(segments)],
+                              0).T for f in range(3)]
+    turned = (turned[0] + turned[1], turned[0] - turned[1], turned[2])
+    for f in range(3):
+        whole = jnp.concatenate([roll(turned[f][LANES - HALO:], pipes, 1), turned[f],
+                                 roll(turned[f][:HALO], -pipes, 1)], 0)
+        fold_ref[0, f, PAD:PAD + rows, :] = whole
+        fold_ref[1, f, PAD:PAD + rows, :] = whole
+
     pl.semaphore_wait(barrier, parts - 1 + slabs - 1)
     copies = []
     for off in range(1, slabs):
@@ -105,83 +149,53 @@
     for copy in copies[:slabs - 1]:
         copy.wait()
 
-    def left_of(x, z):
-        return roll(x, 1, 1)
-
-    def right_of(x, z):
-        return roll(x, -1, 1)
-
-    for half in range(pipes // 8):
-        span = pl.ds(half * 8, 8)
-        own = pl.ds(pl.multiple_of(me * pipes + half * 8, 8), 8)
-        params = all_ref[own, :]
-        drag_c = params[:, DRAG:DRAG + 1]
-        ground_c = params[:, GROUND:GROUND + 1]
-        cool_c = 1.0 / (1.0 + ground_c)
-        for f in range(3):
-            iu_ref[f] = x_ref[f, span, :]
-            iv_ref[f] = x_ref[f, span, :]
-
-        def inner(n, carry):
-            start = tuple(iu_ref[f] for f in range(3))
-            count = count_ref[n]
-            h = 1.0 / count[:, 0:1].astype(jnp.float32)
-            drag_h = h * drag_c
-            cool_h = 1.0 / (1.0 + h * ground_c)
-
-            def step(m, s):
-                return fine_step(s, h, drag_h, cool_h, left_of, right_of)
-
-            def maybe(m, s):
-                live = jnp.concatenate([m < count] * (cells // LANES), 1)
-                return tuple(jnp.where(live, a, b) for a, b in zip(step(m, s), s))
-
-            end = lax.fori_loop(0, STEPS_MIN, step, start)
-            end = lax.fori_loop(STEPS_MIN, STEPS_MAX, maybe, end)
-            guess = coarse_step(start, drag_c, cool_c, left_of, right_of)
-            value = coarse_step(tuple(iv_ref[f] for f in range(3)), drag_c, cool_c,
-                                left_of, right_of)
+    own_pipe = lane % pipes == lax.broadcasted_iota(jnp.int32, (pipes, LANES), 0)
+
+    def in_lanes(ref):
+        return jnp.sum(jnp.where(own_pipe, column(ref[...].reshape(1, pipes)), 0.0), axis=0,
+                       keepdims=True)
+
+    drag = in_lanes(drag_ref)
+    ground = in_lanes(ground_ref)
+    cool = 1.0 / (1.0 + ground)
+    start, value, guess, one, two = (fold_ref.at[k] for k in range(5))
+    chunk = 40
+
+    def inner(n, carry):
+        count = count_ref[n][0:1]
+        h = 1.0 / count.astype(jnp.float32)
+        drag_h = h * drag
+        cool_h = 1.0 / (1.0 + h * ground)
+        sweep(start, [guess], rows, chunk, None, drag, cool)
+        sweep(start, [one], rows, chunk, h, drag_h, cool_h)
+        for source, target in ((one, two), (two, one), (one, two)):
+            sweep(source, [target], rows, chunk, h, drag_h, cool_h)
+
+        def pair(k, c):
+            m = STEPS_MIN + 2 * k
+            sweep(two, [one], rows, chunk, h, drag_h, cool_h, m < count)
+            sweep(one, [two], rows, chunk, h, drag_h, cool_h, m + 1 < count)
+            return c
+
+        lax.fori_loop(0, (STEPS_MAX - STEPS_MIN) // 2, pair, 0)
+        sweep(value, [one], rows, chunk, None, drag, cool)
+        for low in range(PAD, PAD + rows, chunk):
+            part = pl.ds(low, chunk)
             for f in range(3):
-                iu_ref[f] = guess[f]
-                iv_ref[f] = value[f] + (end[f] - guess[f])
-            return carry
-
-        lax.fori_loop(0, slab + 1, inner, 0)
-        for f in range(3):
-            mid_ref[0, f, span, :] = iv_ref[f]
+                coarse = guess[f, part, :]
+                value[f, part, :] = one[f, part, :] + (two[f, part, :] - coarse)
+                start[f, part, :] = coarse
+        return carry
+
+    lax.fori_loop(0, slab + 1, inner, 0)
+    middle = pl.ds(PAD + HALO, LANES)
+    a, b, t = (value[f, middle, :] for f in range(3))
+    for f, x in enumerate((0.5 * (a + b), 0.5 * (a - b), t)):
+        back = x.T
+        for c in range(segments):
+            mid_ref[0, f, :, LANES * c:LANES * (c + 1)] = back[pipes * c:pipes * (c + 1)]
     for copy in copies[slabs - 1:]:
         copy.wait()
-
-
-def coarse_step(state, drag, cool, before, after, z=None):
-    p, q, t = state
-    zl, zr, tl, tr = (None,) * 4 if z is None else z
-    a = before(p + q, zl)
-    b = after(p - q, zr)
-    return finish(0.5 * (a + b), 0.5 * (a - b), q, t, None, drag, cool, before, after, tl, tr)
-
-
-def fine_step(state, h, drag, cool, before, after, z=None):
-    p, q, t = state
-    zl, zr, tl, tr = (None,) * 4 if z is None else z
-    a = p + q
-    b = p - q
-    da = a - before(a, zl)
-    db = b - after(b, zr)
-    half = 0.5 * h
-    return finish(p - half * (da + db), q - half * (da - db), q, t, h, drag, cool, before, after,
-                  tl, tr)
-
-
-def finish(p, r, q, t, h, drag, cool, before, after, tl, tr):
-    slow = 1.0 + jnp.abs(q)
-    dragged = 1.0 + drag * jnp.abs(r)
-    inverse = 1.0 / (slow * dragged)
-    u = q * (dragged * inverse)
-    gain = jnp.maximum(u, 0.0) * (t - before(t, tl)) + jnp.minimum(u, 0.0) * (after(t, tr) - t)
-    if h is not None:
-        gain = h * gain
-    return p, r * (slow * inverse), (t - gain) * cool
 
 
 def solve_kernel(parts, slabs, depth, mid_ref, own_ref, all_ref, steps_ref, out_ref,
@@ -201,13 +215,17 @@
     deep_ref[mine, :] = own_ref[...]
     deep = deep_ref[...].T
     shallow = all_ref[...].T
+    rows = 2 * depth
+    edge = PAD + rows
+    ends = []
     for f in range(3):
         base = 2 * STRIP * f
         near = 2 * extra * f
-        s_ref[0, f, 0:STRIP, :] = shallow[base:base + STRIP]
-        s_ref[0, f, STRIP:depth, :] = deep[near:near + extra]
-        s_ref[0, f, depth:depth + extra, :] = deep[near + extra:near + 2 * extra]
-        s_ref[0, f, depth + extra:2 * depth, :] = shallow[base + STRIP:base + 2 * STRIP]
+        ends.append(jnp.concatenate([
+            shallow[base:base + STRIP], deep[near:near + 2 * extra],
+            shallow[base + STRIP:base + 2 * STRIP]], 0))
+    for f, x in enumerate((ends[0] + ends[1], ends[0] - ends[1], ends[2])):
+        s_ref[0, 0, f, PAD:edge, :] = x
     drag = shallow[DRAG:DRAG + 1]
     ground = shallow[GROUND:GROUND + 1]
 
@@ -216,8 +234,8 @@
     spread = ((source % pipes) == ((target // pipes) % pipes)).astype(f32).astype(bf16)
     table = shallow[TABLE:TABLE + 8]
     owner_of = lax.broadcasted_iota(i32, (8, total), 1) // pipes
-    rows = jnp.concatenate([jnp.where(owner_of == d, table, 0.0) for d in range(parts)], 0)
-    known = jnp.dot(rows.astype(bf16), spread, preferred_element_type=f32)
+    listed = jnp.concatenate([jnp.where(owner_of == d, table, 0.0) for d in range(parts)], 0)
+    known = jnp.dot(listed.astype(bf16), spread, preferred_element_type=f32)
     place = lax.broadcasted_iota(i32, (8 * parts, total), 0)
     known = known + (junctions * (place // 8)).astype(f32)
     names = []
@@ -231,26 +249,18 @@
     adj_ref[...] = meets.astype(bf16)
     inv_ref[...] = 1.0 / jnp.sum(meets, axis=0, keepdims=True)
 
-    last = 2 * depth - 1
-    row_at = lax.broadcasted_iota(i32, (2 * depth, total), 0)
-
-    def before(x, z):
-        return jnp.where(row_at == 0, z, roll(x, 1, 0))
-
-    def after(x, z):
-        return jnp.where(row_at == last, z, roll(x, -1, 0))
-
     def couple(states):
         count = len(states)
         height = -(-2 * count // 8) * 8
         at = lax.broadcasted_iota(i32, (height, 2 * total), 0)
         packed = jnp.zeros((height, 2 * total), f32)
         waves = []
-        for n, (p, q, t) in enumerate(states):
+        for n, state in enumerate(states):
             wave = jnp.concatenate(
-                [p[0:1] - q[0:1], p[last:last + 1] + q[last:last + 1]], 1)
+                [state[1, PAD:PAD + 1, :], state[0, edge - 1:edge, :]], 1)
             waves.append(wave)
-            warmth = jnp.concatenate([t[0:1], t[last:last + 1]], 1)
+            warmth = jnp.concatenate(
+                [state[2, PAD:PAD + 1, :], state[2, edge - 1:edge, :]], 1)
             packed = jnp.where(at == 2 * n, wave, packed)
             packed = jnp.where(at == 2 * n + 1, warmth, packed)
         high = packed.astype(bf16)
@@ -262,12 +272,13 @@
                 + jnp.dot(mid, adj, preferred_element_type=f32)
                 + jnp.dot(high, adj, preferred_element_type=f32))
         means = sums * inv_ref[...]
-        ghosts = []
-        for n in range(count):
+        for n, state in enumerate(states):
             z = 2.0 * means[2 * n:2 * n + 1] - waves[n]
             th = means[2 * n + 1:2 * n + 2]
-            ghosts.append((z[:, :total], z[:, total:], th[:, :total], th[:, total:]))
-        return ghosts
+            state[0, PAD - 1:PAD, :] = z[:, :total]
+            state[1, edge:edge + 1, :] = z[:, total:]
+            state[2, PAD - 1:PAD, :] = th[:, :total]
+            state[2, edge:edge + 1, :] = th[:, total:]
 
     cool_one = 1.0 / (1.0 + ground)
     hs, drags, cools = [], [], []
@@ -277,61 +288,41 @@
         drags.append(h * drag)
         cools.append(1.0 / (1.0 + h * ground))
 
-    def coarse(state, ghosts):
-        return coarse_step(state, drag, cool_one, before, after, ghosts)
-
-    def load(ref, n):
-        return tuple(ref[n, f] for f in range(3))
-
-    def store(ref, n, state):
-        for f in range(3):
-            ref[n, f] = state[f]
-
-    def advance(n, m, state, ghosts):
-        new = fine_step(state, hs[n], drags[n], cools[n], before, after, ghosts)
-        if isinstance(m, int) and m < STEPS_MIN:
-            return new
-        live = m < steps_ref[n, 0, 0]
-        return tuple(jnp.where(live, a, b) for a, b in zip(new, state))
-
-    for t in range(slabs):
-        states = [load(s_ref, n) for n in range(t + 1)]
-        ghosts = couple(states)
-        guess = coarse(states[t], ghosts[t])
-        store(u_ref, t, guess)
-        if t + 1 < slabs:
-            store(s_ref, t + 1, guess)
-        for n in range(t + 1):
-            store(s_ref, n, advance(n, t - n, states[n], ghosts[n]))
-
-    def stage(t, carry):
-        states = [load(s_ref, n) for n in range(slabs)]
-        ghosts = couple(states)
-        for n in range(slabs):
-            store(s_ref, n, advance(n, t - n, states[n], ghosts[n]))
-        return carry
-
-    lax.fori_loop(slabs, STEPS_MAX, stage, 0)
-    value = load(s_ref, 0)
-    store(v_ref, 0, value)
-    for t in range(STEPS_MAX, STEPS_MAX + slabs - 1):
+    chunk = rows // 2
+    last = STEPS_MAX + slabs - 2
+
+    def fine(n, m):
+        return s_ref.at[m % 2, n]
+
+    def advance(n, m, also=()):
+        live = None if m < STEPS_MIN else m < steps_ref[n, 0, 0]
+        sweep(fine(n, m), [fine(n, m + 1), *also], rows, chunk, hs[n], drags[n], cools[n], live)
+
+    for t in range(last + 1):
+        active = [n for n in range(slabs) if 0 <= t - n < STEPS_MAX]
+        states = [fine(n, t - n) for n in active]
         first = t - STEPS_MAX + 1
-        states = [load(s_ref, n) for n in range(first, slabs)]
-        ghosts = couple([value] + states)
-        guess = load(u_ref, first)
-        ends = [advance(n, t - n, states[n - first], ghosts[n - first + 1])
-                for n in range(first, slabs)]
-        for n in range(first + 1, slabs):
-            store(s_ref, n, ends[n - first])
-        value = tuple(g + (e - u) for g, e, u in zip(coarse(value, ghosts[0]), ends[0], guess))
-        store(v_ref, first, value)
+        if first >= 1:
+            value = v_ref.at[first - 1]
+            states.append(value)
+        couple(states)
+        if t < slabs:
+            targets = [u_ref.at[t]] + ([fine(t + 1, 0)] if t + 1 < slabs else [])
+            sweep(fine(t, 0), targets, rows, chunk, None, drag, cool_one)
+        for n in active:
+            advance(n, t - n, [v_ref.at[0]] if n == 0 and t == STEPS_MAX - 1 else [])
+        if first >= 1:
+            sweep(value, [v_ref.at[first]], rows, chunk, None, drag, cool_one)
+            for f in range(3):
+                v_ref[first, f, PAD:edge, :] = v_ref[first, f, PAD:edge, :] + (
+                    s_ref[0, first, f, PAD:edge, :] - u_ref[first, f, PAD:edge, :])
     pieces = []
-    for f in range(3):
-        pieces.append(v_ref[slab, f, 0:STRIP, :])
-        pieces.append(v_ref[slab, f, 2 * depth - STRIP:2 * depth, :])
+    for span in (pl.ds(PAD, STRIP), pl.ds(edge - STRIP, STRIP)):
+        a, b, t = (v_ref[slab, f, span, :] for f in range(3))
+        pieces.append((0.5 * (a + b), 0.5 * (a - b), t))
+    pieces = [side[f] for f in range(3) for side in pieces]
     pieces.append(jnp.zeros((LANES - TABLE, total), f32))
     back_ref[...] = jnp.concatenate(pieces, 0).T
-
     ends = back_ref[mine, :]
     lane = lax.broadcasted_iota(i32, (pipes, LANES), 1)
     for f in range(3):
@@ -359,8 +350,7 @@
                    jax.ShapeDtypeStruct((1, 3, pipes, cells), jnp.float32)),
         in_specs=[vmem] * 5 + [smem],
         out_specs=(vmem,) * 4,
-        scratch_shapes=[pltpu.VMEM((3, 8, cells), jnp.float32),
-                        pltpu.VMEM((3, 8, cells), jnp.float32),
+        scratch_shapes=[pltpu.VMEM((5, 3, LANES + 2 * HALO + 2 * PAD, LANES), jnp.float32),
                         pltpu.SemaphoreType.DMA((parts,)), pltpu.SemaphoreType.DMA((parts,)),
                         pltpu.SemaphoreType.DMA((slabs,)), pltpu.SemaphoreType.DMA((slabs,))],
         compiler_params=pltpu.CompilerParams(collective_id=0, has_side_effects=True),
@@ -373,9 +363,9 @@
         out_specs=vmem,
         scratch_shapes=[
             pltpu.VMEM((total, LANES), jnp.float32),
-            pltpu.VMEM((slabs, 3, 2 * depth, total), jnp.float32),
-            pltpu.VMEM((slabs, 3, 2 * depth, total), jnp.float32),
-            pltpu.VMEM((slabs, 3, 2 * depth, total), jnp.float32),
+            pltpu.VMEM((slabs, 3, 2 * depth + 2 * PAD, total), jnp.float32),
+            pltpu.VMEM((2, slabs, 3, 2 * depth + 2 * PAD, total), jnp.float32),
+            pltpu.VMEM((slabs, 3, 2 * depth + 2 * PAD, total), jnp.float32),
             pltpu.VMEM((2 * total, 2 * total), jnp.bfloat16),
             pltpu.VMEM((1, 2 * total), jnp.float32),
             pltpu.VMEM((total, LANES), jnp.float32),

time: 24.7 us -> 19.4 us (0.79)
  Pallas kernels: 23.8 us -> 18.6 us
    pallas_call x1, Pallas kernels: 18.6 us -> 13.4 us  [body(): pl.pallas_call(functools.partial(gather_kernel, parts, slabs, depth), out...]
where the time goes in v3:
time: 19.4 us; the launch traced here: 19.2 us
  Pallas kernels  18.6 us (96%)
  between operations  0.66 us (3%)
    pallas_call x1, Pallas kernels, body(): pl.pallas_call(functools.partial(gather_kernel, parts, slabs, depth), out...  13.4 us
    pallas_call x1, Pallas kernels, body(): pl.pallas_call(functools.partial(solve_kernel, parts, slabs, depth), out_...  5.15 us

profile of v3, /device:TPU:5, one launch (start us, length us, event | category | flops | bytes accessed | tf_op | source)
XLA Modules:
  0.0 19.2 jit_solution(12453538081402346170)
XLA Ops:
  0.7 13.4 %gather_ends.1 = (f32[128,128]{1,0:T(8,128)}, s32[4,8,128]{2,1,0:T(8,128)}, f32[16,128]{1,0:T(8,128)}, f32[1,3,16,1024]{3,2,1,0:T(8,128)}) custom-call(f32[3,16,1024]{2,1,0:T(8,128)} %x_ref.1, f32[16]{0:T(128)} %drag_ref.1, f32[16]{0:T(128)} %ground_ref.1, s32[1,8,8]{2,1,0:T(8,128)} %send_ref.1, s32[1,8,8]{2,1,0:T(8,128)} %recv_ref.1, s32[1]{0:T(128)S(6)} %copy.7.steps_ref), custom_call_target="tpu_custom_call" | custom-call | tf_op jit(solution)/shard_map/gather_ends/pallas_call | solution.py:345
  14.1 5.2 %solve.1 = f32[1,3,16,1024]{3,2,1,0:T(8,128)} custom-call(f32[1,3,16,1024]{3,2,1,0:T(8,128)} %get-tuple-element.9.mid_ref, f32[16,128]{1,0:T(8,128)} %get-tuple-element.10.own_ref, f32[128,128]{1,0:T(8,128)} %get-tuple-element.11.all_ref, s32[4,8,128]{2,1,0:T(8,128)} %get-tuple-element.12.steps_ref), custom_call_target="tpu_custom_call" | custom-call | tf_op jit(solution)/shard_map/solve/pallas_call | solution.py:359

commit v4 on v3

--- a/solution.py
+++ b/solution.py
@@ -111,8 +111,9 @@
 
     segments = cells // LANES
     rows = LANES + 2 * HALO
-    fold_ref[:, :, 0:PAD, :] = jnp.zeros((5, 3, PAD, LANES), jnp.float32)
-    fold_ref[:, :, PAD + rows:, :] = jnp.zeros((5, 3, PAD, LANES), jnp.float32)
+    buffers = fold_ref.shape[0]
+    fold_ref[:, :, 0:PAD, :] = jnp.zeros((buffers, 3, PAD, LANES), jnp.float32)
+    fold_ref[:, :, PAD + rows:, :] = jnp.zeros((buffers, 3, PAD, LANES), jnp.float32)
     turned = [jnp.concatenate([x_ref[f, :, LANES * c:LANES * (c + 1)] for c in range(segments)],
                               0).T for f in range(3)]
     turned = (turned[0] + turned[1], turned[0] - turned[1], turned[2])
@@ -120,7 +121,25 @@
         whole = jnp.concatenate([roll(turned[f][LANES - HALO:], pipes, 1), turned[f],
                                  roll(turned[f][:HALO], -pipes, 1)], 0)
         fold_ref[0, f, PAD:PAD + rows, :] = whole
-        fold_ref[1, f, PAD:PAD + rows, :] = whole
+        fold_ref[slabs + 1, f, PAD:PAD + rows, :] = whole
+
+    own_pipe = (lane & (pipes - 1)) == lax.broadcasted_iota(jnp.int32, (pipes, LANES), 0)
+
+    def in_lanes(ref):
+        return jnp.sum(jnp.where(own_pipe, column(ref[...].reshape(1, pipes)), 0.0), axis=0,
+                       keepdims=True)
+
+    drag = in_lanes(drag_ref)
+    ground = in_lanes(ground_ref)
+    cool = 1.0 / (1.0 + ground)
+    value, own_end, one, two = (fold_ref.at[slabs + 1 + k] for k in range(4))
+    chunk = 40
+
+    def guess(n, carry):
+        sweep(fold_ref.at[n], [fold_ref.at[n + 1]], rows, chunk, None, drag, cool)
+        return carry
+
+    lax.fori_loop(0, slab + 1, guess, 0)
 
     pl.semaphore_wait(barrier, parts - 1 + slabs - 1)
     copies = []
@@ -146,48 +165,42 @@
         block = jnp.where((lane >= base) & (lane < base + extra), left, block)
         block = jnp.where((lane >= base + extra) & (lane < base + 2 * extra), right, block)
     deep_ref[...] = block
-    for copy in copies[:slabs - 1]:
-        copy.wait()
-
-    own_pipe = lane % pipes == lax.broadcasted_iota(jnp.int32, (pipes, LANES), 0)
-
-    def in_lanes(ref):
-        return jnp.sum(jnp.where(own_pipe, column(ref[...].reshape(1, pipes)), 0.0), axis=0,
-                       keepdims=True)
-
-    drag = in_lanes(drag_ref)
-    ground = in_lanes(ground_ref)
-    cool = 1.0 / (1.0 + ground)
-    start, value, guess, one, two = (fold_ref.at[k] for k in range(5))
-    chunk = 40
-
-    def inner(n, carry):
+    def fine(n, target):
         count = count_ref[n][0:1]
         h = 1.0 / count.astype(jnp.float32)
         drag_h = h * drag
         cool_h = 1.0 / (1.0 + h * ground)
-        sweep(start, [guess], rows, chunk, None, drag, cool)
-        sweep(start, [one], rows, chunk, h, drag_h, cool_h)
-        for source, target in ((one, two), (two, one), (one, two)):
-            sweep(source, [target], rows, chunk, h, drag_h, cool_h)
+        sweep(fold_ref.at[n], [one], rows, chunk, h, drag_h, cool_h)
+        for source, sink in ((one, target), (target, one), (one, target)):
+            sweep(source, [sink], rows, chunk, h, drag_h, cool_h)
 
         def pair(k, c):
             m = STEPS_MIN + 2 * k
-            sweep(two, [one], rows, chunk, h, drag_h, cool_h, m < count)
-            sweep(one, [two], rows, chunk, h, drag_h, cool_h, m + 1 < count)
+            sweep(target, [one], rows, chunk, h, drag_h, cool_h, m < count)
+            sweep(one, [target], rows, chunk, h, drag_h, cool_h, m + 1 < count)
             return c
 
         lax.fori_loop(0, (STEPS_MAX - STEPS_MIN) // 2, pair, 0)
+
+    def correct(n, end):
         sweep(value, [one], rows, chunk, None, drag, cool)
         for low in range(PAD, PAD + rows, chunk):
             part = pl.ds(low, chunk)
             for f in range(3):
-                coarse = guess[f, part, :]
-                value[f, part, :] = one[f, part, :] + (two[f, part, :] - coarse)
-                start[f, part, :] = coarse
+                value[f, part, :] = one[f, part, :] + (
+                    end[f, part, :] - fold_ref[n + 1, f, part, :])
+
+    fine(slab, own_end)
+    for copy in copies[:slabs - 1]:
+        copy.wait()
+
+    def inner(n, carry):
+        fine(n, two)
+        correct(n, two)
         return carry
 
-    lax.fori_loop(0, slab + 1, inner, 0)
+    lax.fori_loop(0, slab, inner, 0)
+    correct(slab, own_end)
     middle = pl.ds(PAD + HALO, LANES)
     a, b, t = (value[f, middle, :] for f in range(3))
     for f, x in enumerate((0.5 * (a + b), 0.5 * (a - b), t)):
@@ -229,15 +242,16 @@
     drag = shallow[DRAG:DRAG + 1]
     ground = shallow[GROUND:GROUND + 1]
 
+    bits = pipes.bit_length() - 1
     source = lax.broadcasted_iota(i32, (total, total), 0)
     target = lax.broadcasted_iota(i32, (total, total), 1)
-    spread = ((source % pipes) == ((target // pipes) % pipes)).astype(f32).astype(bf16)
+    spread = ((source & (pipes - 1)) == ((target >> bits) & (pipes - 1))).astype(f32).astype(bf16)
     table = shallow[TABLE:TABLE + 8]
-    owner_of = lax.broadcasted_iota(i32, (8, total), 1) // pipes
+    owner_of = lax.broadcasted_iota(i32, (8, total), 1) >> bits
     listed = jnp.concatenate([jnp.where(owner_of == d, table, 0.0) for d in range(parts)], 0)
     known = jnp.dot(listed.astype(bf16), spread, preferred_element_type=f32)
     place = lax.broadcasted_iota(i32, (8 * parts, total), 0)
-    known = known + (junctions * (place // 8)).astype(f32)
+    known = known + (junctions * (place >> 3)).astype(f32)
     names = []
     for at in (CODE_LEFT, CODE_RIGHT):
         hit = place.astype(f32) == shallow[at:at + 1]
@@ -263,14 +277,12 @@
                 [state[2, PAD:PAD + 1, :], state[2, edge - 1:edge, :]], 1)
             packed = jnp.where(at == 2 * n, wave, packed)
             packed = jnp.where(at == 2 * n + 1, warmth, packed)
-        high = packed.astype(bf16)
-        rest = packed - high.astype(f32)
-        mid = rest.astype(bf16)
-        low = (rest - mid.astype(f32)).astype(bf16)
-        adj = adj_ref[...]
-        sums = (jnp.dot(low, adj, preferred_element_type=f32)
-                + jnp.dot(mid, adj, preferred_element_type=f32)
-                + jnp.dot(high, adj, preferred_element_type=f32))
+        high = packed.astype(bf16).astype(f32)
+        rest = packed - high
+        mid = rest.astype(bf16).astype(f32)
+        split = jnp.concatenate([rest - mid, mid, high], 0).astype(bf16)
+        sums = jnp.dot(split, adj_ref[...], preferred_element_type=f32)
+        sums = sums[:height] + sums[height:2 * height] + sums[2 * height:]
         means = sums * inv_ref[...]
         for n, state in enumerate(states):
             z = 2.0 * means[2 * n:2 * n + 1] - waves[n]
@@ -350,7 +362,7 @@
                    jax.ShapeDtypeStruct((1, 3, pipes, cells), jnp.float32)),
         in_specs=[vmem] * 5 + [smem],
         out_specs=(vmem,) * 4,
-        scratch_shapes=[pltpu.VMEM((5, 3, LANES + 2 * HALO + 2 * PAD, LANES), jnp.float32),
+        scratch_shapes=[pltpu.VMEM((slabs + 5, 3, LANES + 2 * HALO + 2 * PAD, LANES), jnp.float32),
                         pltpu.SemaphoreType.DMA((parts,)), pltpu.SemaphoreType.DMA((parts,)),
                         pltpu.SemaphoreType.DMA((slabs,)), pltpu.SemaphoreType.DMA((slabs,))],
         compiler_params=pltpu.CompilerParams(collective_id=0, has_side_effects=True),

time: 19.4 us -> 17.5 us (0.902)
  Pallas kernels: 18.6 us -> 16.7 us
    pallas_call x1, Pallas kernels: 13.4 us -> 12.2 us  [body(): pl.pallas_call(functools.partial(gather_kernel, parts, slabs, depth), out...]
    pallas_call x1, Pallas kernels: 5.15 us -> 4.47 us  [body(): pl.pallas_call(functools.partial(solve_kernel, parts, slabs, depth), out_...]
where the time goes in v4:
time: 17.5 us; the launch traced here: 17.4 us
  Pallas kernels  16.7 us (95%)
  between operations  0.66 us (4%)
    pallas_call x1, Pallas kernels, body(): pl.pallas_call(functools.partial(gather_kernel, parts, slabs, depth), out...  12.2 us
    pallas_call x1, Pallas kernels, body(): pl.pallas_call(functools.partial(solve_kernel, parts, slabs, depth), out_...  4.47 us

profile of v4, /device:TPU:5, one launch (start us, length us, event | category | flops | bytes accessed | tf_op | source)
XLA Modules:
  0.0 17.4 jit_solution(9452789309874434632)
XLA Ops:
  0.7 12.2 %gather_ends.1 = (f32[128,128]{1,0:T(8,128)}, s32[4,8,128]{2,1,0:T(8,128)}, f32[16,128]{1,0:T(8,128)}, f32[1,3,16,1024]{3,2,1,0:T(8,128)}) custom-call(f32[3,16,1024]{2,1,0:T(8,128)} %x_ref.1, f32[16]{0:T(128)} %drag_ref.1, f32[16]{0:T(128)} %ground_ref.1, s32[1,8,8]{2,1,0:T(8,128)} %send_ref.1, s32[1,8,8]{2,1,0:T(8,128)} %recv_ref.1, s32[1]{0:T(128)S(6)} %copy.7.steps_ref), custom_call_target="tpu_custom_call" | custom-call | tf_op jit(solution)/shard_map/gather_ends/pallas_call | solution.py:357
  12.9 4.5 %solve.1 = f32[1,3,16,1024]{3,2,1,0:T(8,128)} custom-call(f32[1,3,16,1024]{3,2,1,0:T(8,128)} %get-tuple-element.9.mid_ref, f32[16,128]{1,0:T(8,128)} %get-tuple-element.10.own_ref, f32[128,128]{1,0:T(8,128)} %get-tuple-element.11.all_ref, s32[4,8,128]{2,1,0:T(8,128)} %get-tuple-element.12.steps_ref), custom_call_target="tpu_custom_call" | custom-call | tf_op jit(solution)/shard_map/solve/pallas_call | solution.py:371

commit v5 on v4

--- a/solution.py
+++ b/solution.py
@@ -107,7 +107,7 @@
         all_ref[pl.ds(pl.multiple_of(me * pipes, pipes), rows),
                 TABLE + g * slots:TABLE + (g + 1) * slots] = (
             recv_ref[0, g * pipes:g * pipes + rows, :].astype(jnp.float32))
-    count_ref[slab] = jnp.full((8, LANES), steps_ref[0], jnp.int32)
+    count_ref[slab] = jnp.broadcast_to(steps_ref[...].reshape(1, 1), (8, LANES))
 
     segments = cells // LANES
     rows = LANES + 2 * HALO
@@ -165,6 +165,7 @@
         block = jnp.where((lane >= base) & (lane < base + extra), left, block)
         block = jnp.where((lane >= base + extra) & (lane < base + 2 * extra), right, block)
     deep_ref[...] = block
+
     def fine(n, target):
         count = count_ref[n][0:1]
         h = 1.0 / count.astype(jnp.float32)
@@ -293,9 +294,11 @@
             state[2, edge:edge + 1, :] = th[:, total:]
 
     cool_one = 1.0 / (1.0 + ground)
-    hs, drags, cools = [], [], []
+    counts, hs, drags, cools = [], [], [], []
     for n in range(slabs):
-        h = 1.0 / (jnp.zeros((1, total), f32) + steps_ref[n, 0, 0].astype(f32))
+        count = jnp.concatenate([steps_ref[n][0:1]] * (total // LANES), 1)
+        h = 1.0 / count.astype(f32)
+        counts.append(count)
         hs.append(h)
         drags.append(h * drag)
         cools.append(1.0 / (1.0 + h * ground))
@@ -307,7 +310,7 @@
         return s_ref.at[m % 2, n]
 
     def advance(n, m, also=()):
-        live = None if m < STEPS_MIN else m < steps_ref[n, 0, 0]
+        live = None if m < STEPS_MIN else m < counts[n]
         sweep(fine(n, m), [fine(n, m + 1), *also], rows, chunk, hs[n], drags[n], cools[n], live)
 
     for t in range(last + 1):
@@ -353,14 +356,13 @@
     total = parts * pipes
     depth = -(-2 * (slabs + STEPS_MAX - 1) // 8) * 8
     vmem = pl.BlockSpec(memory_space=pltpu.VMEM)
-    smem = pl.BlockSpec(memory_space=pltpu.SMEM)
     gathered, counts, own, mid = pl.pallas_call(
         functools.partial(gather_kernel, parts, slabs, depth),
         out_shape=(jax.ShapeDtypeStruct((total, LANES), jnp.float32),
                    jax.ShapeDtypeStruct((slabs, 8, LANES), jnp.int32),
                    jax.ShapeDtypeStruct((pipes, LANES), jnp.float32),
                    jax.ShapeDtypeStruct((1, 3, pipes, cells), jnp.float32)),
-        in_specs=[vmem] * 5 + [smem],
+        in_specs=[vmem] * 6,
         out_specs=(vmem,) * 4,
         scratch_shapes=[pltpu.VMEM((slabs + 5, 3, LANES + 2 * HALO + 2 * PAD, LANES), jnp.float32),
                         pltpu.SemaphoreType.DMA((parts,)), pltpu.SemaphoreType.DMA((parts,)),
@@ -371,7 +373,7 @@
     return pl.pallas_call(
         functools.partial(solve_kernel, parts, slabs, depth),
         out_shape=jax.ShapeDtypeStruct((1, 3, pipes, cells), jnp.float32),
-        in_specs=[vmem, vmem, vmem, smem],
+        in_specs=[vmem] * 4,
         out_specs=vmem,
         scratch_shapes=[
             pltpu.VMEM((total, LANES), jnp.float32),

time: 17.5 us -> 17.4 us (level)
  no operation moved by 1% of the time
where the time goes in v5:
time: 17.4 us; the launch traced here: 17.3 us
  Pallas kernels  16.6 us (95%)
  between operations  0.66 us (4%)
    pallas_call x1, Pallas kernels, body(): pl.pallas_call(functools.partial(gather_kernel, parts, slabs, depth), out...  12.2 us
    pallas_call x1, Pallas kernels, body(): pl.pallas_call(functools.partial(solve_kernel, parts, slabs, depth), out_...  4.41 us

profile of v5, /device:TPU:5, one launch (start us, length us, event | category | flops | bytes accessed | tf_op | source)
XLA Modules:
  0.0 17.3 jit_solution(17418146424377458958)
XLA Ops:
  0.7 12.2 %gather_ends.1 = (f32[128,128]{1,0:T(8,128)}, s32[4,8,128]{2,1,0:T(8,128)}, f32[16,128]{1,0:T(8,128)}, f32[1,3,16,1024]{3,2,1,0:T(8,128)}) custom-call(f32[3,16,1024]{2,1,0:T(8,128)} %x_ref.1, f32[16]{0:T(128)} %drag_ref.1, f32[16]{0:T(128)} %ground_ref.1, s32[1,8,8]{2,1,0:T(8,128)} %send_ref.1, s32[1,8,8]{2,1,0:T(8,128)} %recv_ref.1, s32[1]{0:T(128)S(6)} %copy.7.steps_ref), custom_call_target="tpu_custom_call" | custom-call | tf_op jit(solution)/shard_map/gather_ends/pallas_call | solution.py:359
  12.9 4.4 %solve.1 = f32[1,3,16,1024]{3,2,1,0:T(8,128)} custom-call(f32[1,3,16,1024]{3,2,1,0:T(8,128)} %get-tuple-element.9.mid_ref, f32[16,128]{1,0:T(8,128)} %get-tuple-element.10.own_ref, f32[128,128]{1,0:T(8,128)} %get-tuple-element.11.all_ref, s32[4,8,128]{2,1,0:T(8,128)} %get-tuple-element.12.steps_ref), custom_call_target="tpu_custom_call" | custom-call | tf_op jit(solution)/shard_map/solve/pallas_call | solution.py:373
